TPU v7x, 128 devices: a whole 4x4x4 slice. The times are simulated.
128 devices in a mesh: blk: 32 (over x, z, y_lo), group: 4 (over y_hi, core).
Axes of the slice: x: 4, y: 4 (y_hi: 2, y_lo: 2; y = y_hi * 2 + y_lo), z: 4, core: 2. Of those that a mesh axis runs over, the one named last changes fastest.
Arguments:
- queries: bfloat16 [32, 2048, 2560], P('blk', 'group'), may hold values from -6 to 6
- new_keys: bfloat16 [32, 2048, 256], P('blk', 'group'), may hold values from -15 to 15
- new_values: bfloat16 [32, 2048, 256], P('blk', 'group'), may hold values from -4 to 4
- key_cache: bfloat16 [1280, 128, 256], P('blk', 'group'), may hold values from -4 to 4
- value_cache: bfloat16 [1280, 128, 256], P('blk', 'group'), may hold values from -4 to 4
- out_weight: bfloat16 [2560, 2560], replicated, may hold values from -0.375 to 0.375
- lengths: int32 [32], replicated, may hold values from 0 to 30720, as said below
- page_table: int32 [32, 32], replicated, may hold values from 0 to 1279, as said below
Outputs:
- hidden_states: bfloat16 [32, 2048, 2560], P('blk', 'group')
- key_cache_out: bfloat16 [1280, 128, 256], P('blk', 'group')
- value_cache_out: bfloat16 [1280, 128, 256], P('blk', 'group')
Inputs may be any that keep to these rules, and one draw needn't show every extreme that they name: `lengths`: multiples of 2048; some request has length 0 and some has 30720. `page_table`: all entries differ; page p lies on blk index p // 40; columns below 16 hold the request's last 16 pages before its group in order (pages that hold no part of a request where its length is short), the others the pages of its group in order; of one request's first 16 entries at most 1 lie on one blk index, of its last 16 at most 1, and both bounds are reached for every request.
All inputs are finite; a program needn't handle non-finite values.
Results may differ from a plain program's by a relative error of at most 0.009.
Values may be sent and summed in bfloat16 or wider, within the bound.
A program may use at most 256 MiB of HBM per device.

v0:
```python
import jax
import jax.numpy as jnp
from jax import lax
from jax.sharding import PartitionSpec as P

masked_score = -1e30
key_block_size = 512


def rotate(values, positions):
    quarter = values.shape[-1] // 4
    freq_table = 10000.0 ** (-jnp.arange(quarter, dtype=jnp.float32) / quarter)
    angles = positions.astype(jnp.float32)[..., None] * freq_table
    cosine = jnp.cos(angles)
    sine_part = jnp.sin(angles)
    leading = values[..., :quarter]
    trailing = values[..., quarter : 2 * quarter]
    return jnp.concatenate(
        [
            leading * cosine - trailing * sine_part,
            trailing * cosine + leading * sine_part,
            values[..., 2 * quarter :],
        ],
        axis=-1,
    )


def attend_block(carried, query_block, key_rows, value_rows, visible, score_scale):
    running_max, running_sum, running_acc = carried
    scores = (
        jnp.einsum("thd,kd->thk", query_block, key_rows, preferred_element_type=jnp.float32)
        * score_scale
    )
    scores = jnp.where(visible, scores, masked_score)
    new_max = jnp.maximum(running_max, jnp.max(scores, axis=2))
    weights = jnp.where(visible, jnp.exp(scores - new_max[:, :, None]), 0.0)
    factor = jnp.exp(running_max - new_max)
    new_sum = running_sum * factor + jnp.sum(weights, axis=2)
    new_acc = running_acc * factor[:, :, None] + jnp.einsum(
        "thk,kd->thd", weights.astype(jnp.bfloat16), value_rows, preferred_element_type=jnp.float32
    )
    return (new_max, new_sum, new_acc)


def attend(carried, query_block, key_rows, value_rows, visible, score_scale):
    key_total = key_rows.shape[0]
    for block_start in range(0, key_total, key_block_size):
        block_stop = min(block_start + key_block_size, key_total)
        carried = attend_block(
            carried,
            query_block,
            key_rows[block_start:block_stop],
            value_rows[block_start:block_stop],
            visible[:, :, block_start:block_stop],
            score_scale,
        )
    return carried


def body(queries, new_keys, new_values, key_cache, value_cache, out_weight, lengths, page_table):
    blk_count = lax.axis_size("blk")
    blk_index = lax.axis_index("blk")
    group_count = lax.axis_size("group")
    group_index = lax.axis_index("group")
    tok_rows = queries.shape[1]
    head_dim = new_keys.shape[2]
    head_count = queries.shape[2] // head_dim
    pages_here = key_cache.shape[0]
    page_rows = key_cache.shape[1]
    page_len = page_rows * group_count
    slot_count = page_table.shape[1]
    group_len = tok_rows * group_count
    fresh_pages = group_len // page_len
    window_pages = slot_count - fresh_pages
    window_len = window_pages * page_len
    score_scale = head_dim ** (-0.5)
    length = lengths[blk_index]
    my_table = page_table[blk_index]
    offsets = group_index * tok_rows + jnp.arange(tok_rows, dtype=jnp.int32)
    positions = length + offsets
    roped_queries = rotate(
        queries[0].astype(jnp.float32).reshape(tok_rows, head_count, head_dim), positions[:, None]
    ).astype(jnp.bfloat16)
    roped_keys = rotate(new_keys[0].astype(jnp.float32), positions).astype(jnp.bfloat16)
    all_keys, all_values = (
        lax.all_gather(roped_keys, "group", axis=0, tiled=True),
        lax.all_gather(new_values[0], "group", axis=0, tiled=True),
    )
    key_index = jnp.arange(group_len, dtype=jnp.int32)
    fresh_visible = key_index[None, :] <= offsets[:, None]
    initial = (
        jnp.full((tok_rows, head_count), masked_score, jnp.float32),
        jnp.zeros((tok_rows, head_count), jnp.float32),
        jnp.zeros((tok_rows, head_count, head_dim), jnp.float32),
    )
    carried = attend(
        initial, roped_queries, all_keys, all_values, fresh_visible[:, None, :], score_scale
    )
    old_table = my_table[:window_pages]
    blank_pages = jnp.zeros((window_pages, page_rows, head_dim), jnp.bfloat16)
    pieces = (
        lax.all_gather(key_cache, "blk", axis=0, tiled=True),
        lax.all_gather(value_cache, "blk", axis=0, tiled=True),
    )
    held_pages = pieces[0].shape[0]
    inside = (old_table >= 0) & (old_table < held_pages)
    clipped = jnp.clip(old_table, 0, held_pages - 1)
    old_keys = jnp.where(inside[:, None, None], pieces[0][clipped], blank_pages)
    old_values = jnp.where(inside[:, None, None], pieces[1][clipped], blank_pages)
    pieces = (
        lax.all_gather(old_keys, "group", axis=1, tiled=True),
        lax.all_gather(old_values, "group", axis=1, tiled=True),
    )
    piece_rows = pieces[0].shape[1]
    key_rows = pieces[0].reshape(-1, head_dim)
    value_rows = pieces[1].reshape(-1, head_dim)
    in_window = (
        jnp.arange(window_pages, dtype=jnp.int32)[:, None] * page_len
        + jnp.arange(piece_rows, dtype=jnp.int32)[None, :]
    ).reshape(-1)
    visible = (in_window[None, :] > offsets[:, None]) & (
        length - window_len + in_window[None, :] >= 0
    )
    carried = attend(carried, roped_queries, key_rows, value_rows, visible[:, None, :], score_scale)
    running_max, running_sum, running_acc = carried
    attended = (
        (running_acc / running_sum[:, :, None])
        .astype(jnp.bfloat16)
        .reshape(tok_rows, head_count * head_dim)
    )
    hidden = jnp.dot(attended, out_weight, preferred_element_type=jnp.float32).astype(jnp.bfloat16)[
        None
    ]
    cap_new = (fresh_pages + blk_count - 1) // blk_count
    quarter_keys = lax.dynamic_index_in_dim(
        all_keys.reshape(fresh_pages, group_count, page_rows, head_dim),
        group_index,
        axis=1,
        keepdims=False,
    )
    quarter_values = lax.dynamic_index_in_dim(
        all_values.reshape(fresh_pages, group_count, page_rows, head_dim),
        group_index,
        axis=1,
        keepdims=False,
    )
    new_owner = my_table[window_pages:] // pages_here
    fresh_ids = jnp.arange(fresh_pages, dtype=jnp.int32)
    before = fresh_ids[None, :] < fresh_ids[:, None]
    new_rank = jnp.sum(
        (before & (new_owner[None, :] == new_owner[:, None])).astype(jnp.int32), axis=1
    )
    placing = (
        (new_owner[None, None, :] == jnp.arange(blk_count, dtype=jnp.int32)[:, None, None])
        & (new_rank[None, None, :] == jnp.arange(cap_new, dtype=jnp.int32)[None, :, None])
    ).astype(jnp.bfloat16)
    send_new_keys = jnp.einsum(
        "ocj,jrd->ocrd", placing, quarter_keys, preferred_element_type=jnp.float32
    ).astype(jnp.bfloat16)
    send_new_values = jnp.einsum(
        "ocj,jrd->ocrd", placing, quarter_values, preferred_element_type=jnp.float32
    ).astype(jnp.bfloat16)
    arrived_keys, arrived_values = (
        lax.all_to_all(send_new_keys, "blk", split_axis=0, concat_axis=0, tiled=True),
        lax.all_to_all(send_new_values, "blk", split_axis=0, concat_axis=0, tiled=True),
    )
    owned_slots = page_table[:, window_pages:] // pages_here == blk_index
    hit_rank = jnp.cumsum(owned_slots.astype(jnp.int32), axis=1) - 1
    choose = owned_slots[:, None, :] & (
        hit_rank[:, None, :] == jnp.arange(cap_new, dtype=jnp.int32)[None, :, None]
    )
    target = jnp.where(
        jnp.any(choose, axis=2),
        jnp.sum(jnp.where(choose, page_table[:, None, window_pages:] % pages_here, 0), axis=2),
        pages_here,
    )
    key_out = key_cache.at[target.reshape(-1)].set(
        arrived_keys.reshape(-1, page_rows, head_dim), mode="drop"
    )
    value_out = value_cache.at[target.reshape(-1)].set(
        arrived_values.reshape(-1, page_rows, head_dim), mode="drop"
    )
    return (hidden, key_out, value_out)


def solution(mesh):
    return jax.shard_map(
        body,
        mesh=mesh,
        in_specs=(
            P("blk", "group", None),
            P("blk", "group", None),
            P("blk", "group", None),
            P("blk", "group", None),
            P("blk", "group", None),
            P(),
            P(),
            P(),
        ),
        out_specs=(P("blk", "group", None), P("blk", "group", None), P("blk", "group", None)),
        check_vma=False,
    )
```

profile of v0, /device:TPU:1, one launch (start us, length us, event | category | flops | bytes accessed | tf_op | source)
XLA Modules:
  0.0 1176.4 jit_solution(8598591531830800221)
XLA Ops:
  46.5 9.9 all-to-all-start
  56.7 11.7 all-gather.18.cloned.1.call-done
  73.2 7.3 fusion.3
  80.5 437.2 %all-gather.10.cloned.1.call-done = bf16[1280,32,256]{2,1,0:T(8,128)(2,1)} async-done(((bf16[40,32,256]{2,1,0:T(8,128)(2,1)}), bf16[1280,32,256]{2,1,0:T(8,128)(2,1)}) %all-gather.10.cloned.1.call-update) | async-done | bytes 20971536 | tf_op jit(solution)/shard_map/all_gather | solution.py:102
  517.7 7.5 gather_fusion
  525.2 443.7 %all-gather.14.cloned.1.call-done = bf16[1280,32,256]{2,1,0:T(8,128)(2,1)} async-done(((bf16[40,32,256]{2,1,0:T(8,128)(2,1)}), bf16[1280,32,256]{2,1,0:T(8,128)(2,1)}) %all-gather.14.cloned.1.call-update) | async-done | bytes 20971536 | tf_op jit(solution)/shard_map/all_gather | solution.py:103
  969.0 7.5 gather_fusion.1
  977.4 7.5 fusion.2
  984.9 7.3 fusion.1
  992.3 10.4 all-to-all-start.1
  1002.7 7.4 fusion
  1017.3 7.4 fusion.4
  1024.7 5.8 fusion.5
  1030.5 5.8 fusion.6
  1046.6 10.0 fusion.24
  1056.6 7.1 fusion.20
  1063.7 9.8 fusion.26
  1076.5 10.1 fusion.28
  1089.8 9.8 fusion.30
  1105.8 7.6 fusion.12
  1118.3 5.6 fusion.32
  1124.0 9.5 fusion.34
  1138.2 19.2 %divide_convert_fusion = bf16[512,10,256]{0,2,1:T(8,128)(2,1)} fusion(f32[512,10,256]{0,2,1:T(8,128)} %fusion.24, f32[512,10,256]{0,2,1:T(8,128)} %fusion.26, f32[512,10,256]{0,2,1:T(8,128)} %fusion.28, f32[512,10,256]{0,2,1:T(8,128)} %fusion.30, f32[512,10,256]{0,2,1:T(8,128)} %fusion.32, f32[512,10,256]{0,2,1:T(8,128)} %fusion.34, ...), kind=kOutput, calls=%fused_computation.52 | convolution fusion | flops 1377566720 | bytes 50536448 | tf_op jit(solution)/shard_map/thk,kd->thd/dot_general | solution.py:39
  1157.4 12.0 %fusion.80 = bf16[1,512,2560]{2,1,0:T(8,128)(2,1)} fusion(bf16[512,2560]{0,1:T(8,128)(2,1)} %bitcast.170, bf16[2560,2560]{1,0:T(8,128)(2,1)} %param.13), kind=kOutput, calls=%fused_computation.96 | convolution fusion | flops 6712197120 | bytes 18350080 | tf_op jit(solution)/shard_map/dot_general | solution.py:131
  (169 shorter events, 83.8 us)
Async XLA Ops:
  7.2 36.8 %all-gather.8.cloned.1.call-start = ((), (), s32[]{:S(2)}) async-start(), calls=%async_computation.2 | async-start | bytes 1310720 | tf_op jit(solution)/shard_map/all_gather | solution.py:86
  17.0 51.4 %all-gather.18.cloned.1.call-start = ((), (), s32[]{:S(2)}) async-start(), calls=%async_computation.7 | async-start | bytes 1310720 | tf_op jit(solution)/shard_map/all_gather | solution.py:87
  18.9 498.8 %all-gather.10.cloned.1.call-start = ((), (), s32[]{:S(2)}) async-start(), calls=%async_computation.3 | async-start | bytes 21626880 | tf_op jit(solution)/shard_map/all_gather | solution.py:102
  19.6 949.4 %all-gather.14.cloned.1.call-start = ((), (), s32[]{:S(2)}) async-start(), calls=%async_computation.5 | async-start | bytes 21626880 | tf_op jit(solution)/shard_map/all_gather | solution.py:103
  39.3 945.7 %copy-start.5 = (bf16[512,10,256]{2,0,1:T(8,128)(2,1)}, bf16[512,10,256]{2,0,1:T(8,128)(2,1)S(1)}, u32[]{:S(2)}) copy-start(bf16[512,10,256]{2,0,1:T(8,128)(2,1)S(1)} %pad_maximum_fusion) | copy-start | bytes 7864324
  42.8 37.7 %copy-start.11 = (pred[512,512]{0,1:T(8,128)(4,1)}, pred[512,512]{0,1:T(8,128)(4,1)S(1)}, u32[]{:S(2)}) copy-start(pred[512,512]{0,1:T(8,128)(4,1)S(1)} %get-tuple-element.31) | copy-start | bytes 786436
  46.5 945.8 %all-to-all-start = ((bf16[32,1,32,256]{3,2,1,0:T(8,128)(2,1)}), bf16[32,1,32,256]{3,2,1,0:T(8,128)(2,1)}, u32[]{:S(2)}, u32[]{:S(2)}) async-start(bf16[32,1,32,256]{3,2,1,0:T(8,128)(2,1)} %copy.87), calls=%async_computation | async-start | bytes 1048576 | tf_op jit(solution)/shard_map/all_to_all | solution.py:164
  56.3 959.4 %all-gather.12.cloned.1.call-start = ((), (), s32[]{:S(2)}) async-start(), calls=%async_computation.4 | async-start | bytes 1310720 | tf_op jit(solution)/shard_map/all_gather | solution.py:111
  992.2 17.9 %copy-start.3 = (bf16[40,32,256]{2,1,0:T(8,128)(2,1)S(1)}, bf16[40,32,256]{2,1,0:T(8,128)(2,1)}, u32[]{:S(2)}) copy-start(bf16[40,32,256]{2,1,0:T(8,128)(2,1)} %copy.115) | copy-start | bytes 1966084
  992.2 21.4 %copy-start.1 = (bf16[40,32,256]{2,1,0:T(8,128)(2,1)S(1)}, bf16[40,32,256]{2,1,0:T(8,128)(2,1)}, u32[]{:S(2)}) copy-start(bf16[40,32,256]{2,1,0:T(8,128)(2,1)} %copy.116) | copy-start | bytes 1966084
  992.3 21.3 %all-to-all-start.1 = ((bf16[32,1,32,256]{3,2,1,0:T(8,128)(2,1)}), bf16[32,1,32,256]{3,2,1,0:T(8,128)(2,1)S(1)}, u32[]{:S(2)}, u32[]{:S(2)}) async-start(bf16[32,1,32,256]{3,2,1,0:T(8,128)(2,1)} %copy.90), calls=%async_computation.1 | async-start | bytes 1048576 | tf_op jit(solution)/shard_map/all_to_all | solution.py:165
  1002.7 42.6 %all-gather.16.cloned.1.call-start = ((), (), s32[]{:S(2)}) async-start(), calls=%async_computation.6 | async-start | bytes 1310720 | tf_op jit(solution)/shard_map/all_gather | solution.py:112
  1010.2 28.0 %copy-start.25 = (f32[512,10]{0,1:T(8,128)}, f32[512,10]{0,1:T(8,128)S(1)}, u32[]{:S(2)}) copy-start(f32[512,10]{0,1:T(8,128)S(1)} %get-tuple-element.66) | copy-start | bytes 61444
  1039.0 24.6 %copy-start.21 = (f32[512,10]{0,1:T(8,128)}, f32[512,10]{0,1:T(8,128)S(1)}, u32[]{:S(2)}) copy-start(f32[512,10]{0,1:T(8,128)S(1)} %get-tuple-element.18) | copy-start | bytes 61444
  1039.0 37.5 %copy-start.22 = (f32[512,10]{0,1:T(8,128)}, f32[512,10]{0,1:T(8,128)S(1)}, u32[]{:S(2)}) copy-start(f32[512,10]{0,1:T(8,128)S(1)} %get-tuple-element.19) | copy-start | bytes 61444
  1039.0 50.7 %copy-start.23 = (f32[512,10]{0,1:T(8,128)}, f32[512,10]{0,1:T(8,128)S(1)}, u32[]{:S(2)}) copy-start(f32[512,10]{0,1:T(8,128)S(1)} %get-tuple-element.20) | copy-start | bytes 61444
  1039.0 60.6 %copy-start.24 = (f32[512,10]{0,1:T(8,128)}, f32[512,10]{0,1:T(8,128)S(1)}, u32[]{:S(2)}) copy-start(f32[512,10]{0,1:T(8,128)S(1)} %get-tuple-element.45) | copy-start | bytes 61444
  1039.0 63.7 %copy-start.19 = (f32[512,10]{0,1:T(8,128)}, f32[512,10]{0,1:T(8,128)S(1)}, u32[]{:S(2)}) copy-start(f32[512,10]{0,1:T(8,128)S(1)} %get-tuple-element.21) | copy-start | bytes 61444
  1046.5 26.9 %slice-start.12 = ((s8[10485760]{0:T(1024)(128)(4,1)}), s8[4194304]{0:T(1024)(128)(4,1)S(1)}, s32[]{:S(2)}) async-start(s8[10485760]{0:T(1024)(128)(4,1)} %bitcast.155), calls=%async_computation.20 | async-start | bytes 8388608
  1046.5 26.9 %slice-start.13 = ((s8[10485760]{0:T(1024)(128)(4,1)}), s8[4194304]{0:T(1024)(128)(4,1)S(1)}, s32[]{:S(2)}) async-start(s8[10485760]{0:T(1024)(128)(4,1)} %bitcast.155), calls=%async_computation.21 | async-start | bytes 8388608
  1063.6 23.0 %slice-start.9 = ((s8[10485760]{0:T(1024)(128)(4,1)}), s8[4194304]{0:T(1024)(128)(4,1)S(1)}, s32[]{:S(2)}) async-start(s8[10485760]{0:T(1024)(128)(4,1)} %bitcast.153), calls=%async_computation.17 | async-start | bytes 8388608
  1063.6 23.0 %slice-start.10 = ((s8[10485760]{0:T(1024)(128)(4,1)}), s8[4194304]{0:T(1024)(128)(4,1)S(1)}, s32[]{:S(2)}) async-start(s8[10485760]{0:T(1024)(128)(4,1)} %bitcast.153), calls=%async_computation.18 | async-start | bytes 8388608
  1076.5 23.0 %slice-start.6 = ((s8[10485760]{0:T(1024)(128)(4,1)}), s8[4194304]{0:T(1024)(128)(4,1)S(1)}, s32[]{:S(2)}) async-start(s8[10485760]{0:T(1024)(128)(4,1)} %bitcast.151), calls=%async_computation.14 | async-start | bytes 8388608
  1076.5 23.0 %slice-start.7 = ((s8[10485760]{0:T(1024)(128)(4,1)}), s8[4194304]{0:T(1024)(128)(4,1)S(1)}, s32[]{:S(2)}) async-start(s8[10485760]{0:T(1024)(128)(4,1)} %bitcast.151), calls=%async_computation.15 | async-start | bytes 8388608
  (29 other events, 266.8 us)
Sparse Core Ops, SparseCore 0:
  17.1 24.3 all-gather.7
  43.2 25.1 all-gather.17
  70.6 447.0 all-gather.9
  519.2 449.7 all-gather.13
  977.6 23.4 all-gather.11
  1015.9 21.4 all-gather.15
where the time goes:
time: 1180 us
  waiting for transfers between devices  894 us (76%)
  matrix products  142 us (12%)
  other arithmetic  52.3 us (4%)
  local copies, waits for them, and re-layouts  51.9 us (4%)
  starting transfers between devices  20.8 us (2%)
  between operations  15.4 us (1%)
    all_gather x1, waiting for transfers between devices, body(): lax.all_gather(value_cache, 'blk', axis=0, tiled=True)  444 us
    all_gather x1, waiting for transfers between devices, body(): lax.all_gather(key_cache, 'blk', axis=0, tiled=True)  437 us
    dot_general x8, matrix products, attend_block(): jnp.einsum('thk,kd->thd', weights.astype(jnp.bfloat16), value_rows, prefe...  78.7 us
    dot_general x8, matrix products, attend_block(): jnp.einsum('thd,kd->thk', query_block, key_rows, preferred_element_type=j...  50.4 us
    reduce_sum x8, other arithmetic, attend_block(): new_sum = running_sum * factor + jnp.sum(weights, axis=2)  33.2 us
  transfers between devices with their start and end apart: 8, of which 3 were waited for; matrix products, arithmetic and copies ran while one was open for 9% of the time, Pallas kernels for 0%

commit v1 on v0

v1 whole, which is shorter than its diff:
```python
import functools

import jax
import jax.numpy as jnp
from jax import lax
from jax.experimental import pallas as pl
from jax.experimental.pallas import tpu as pltpu
from jax.sharding import PartitionSpec as P

MESH = pl.DeviceIdType.MESH
NEG = -1e30
ANY = pl.BlockSpec(memory_space=pl.ANY)
VM = pl.BlockSpec(memory_space=pltpu.VMEM)
SM = pl.BlockSpec(memory_space=pltpu.SMEM)


def rope_tables(positions, quarter):
    freq_table = 10000.0 ** (-jnp.arange(quarter, dtype=jnp.float32) / quarter)
    angles = positions.astype(jnp.float32)[..., None] * freq_table
    cosine, sine = jnp.cos(angles), jnp.sin(angles)
    return (
        jnp.concatenate([cosine, cosine], axis=-1),
        jnp.concatenate([-sine, sine], axis=-1),
    )


def comm_kernel(
    dims,
    tab,
    fresh_k,
    fresh_v,
    kcache,
    vcache,
    kwin,
    vwin,
    newrecv,
    send_old,
    recv_old,
    comp_k,
    comp_v,
    qbuf_k,
    qbuf_v,
    send_new,
    s_old,
    r_old,
    s_fr,
    r_fr,
    s_q,
    r_q,
    s_ag,
    r_ag,
    s_new,
    r_new,
    loc,
):
    nb, ng, old_pages, mine = dims
    me = lax.axis_index("blk")
    g = lax.axis_index("group")

    barrier = pltpu.get_barrier_semaphore()

    def greet(k, _):
        pl.semaphore_signal(
            barrier, inc=1, device_id={"blk": lax.rem(me + k, nb), "group": g}, device_id_type=MESH
        )
        return 0

    lax.fori_loop(1, nb, greet, 0)
    for d in range(1, ng):
        pl.semaphore_signal(
            barrier, inc=1, device_id={"blk": me, "group": lax.rem(g + d, ng)}, device_id_type=MESH
        )

    def fill(a, _):
        i = tab[0, a]
        send_old[a, 0] = kcache[i]
        send_old[a, 1] = vcache[i]
        return 0

    lax.fori_loop(0, nb, fill, 0)
    recv_old[me] = send_old[me]
    pl.semaphore_wait(barrier, nb - 1 + ng - 1)

    def old_copy(k):
        a = lax.rem(me + k, nb)
        return pltpu.make_async_remote_copy(
            src_ref=send_old.at[a],
            dst_ref=recv_old.at[me],
            send_sem=s_old.at[a],
            recv_sem=r_old.at[me],
            device_id={"blk": a, "group": g},
            device_id_type=MESH,
        )

    def old_landed(k):
        a = lax.rem(me + nb - k, nb)
        return pltpu.make_async_remote_copy(
            src_ref=send_old.at[a],
            dst_ref=recv_old.at[a],
            send_sem=s_old.at[a],
            recv_sem=r_old.at[a],
            device_id={"blk": a, "group": g},
            device_id_type=MESH,
        )

    def start_old(k, _):
        old_copy(k).start()
        return 0

    lax.fori_loop(1, nb, start_old, 0)

    def quarter_copies(d):
        peer = lax.rem(g + d, ng)
        return [
            pltpu.make_async_remote_copy(
                src_ref=src.at[:, peer],
                dst_ref=dst.at[pl.ds(g * mine, mine)],
                send_sem=s_q.at[d, n],
                recv_sem=r_q.at[d, n],
                device_id={"blk": me, "group": peer},
                device_id_type=MESH,
            )
            for n, (src, dst) in enumerate(((fresh_k, qbuf_k), (fresh_v, qbuf_v)))
        ]

    def fresh_copies(d):
        peer = lax.rem(g + d, ng)
        return [
            pltpu.make_async_remote_copy(
                src_ref=src,
                dst_ref=dst.at[pl.ds(old_pages + g * mine, mine)],
                send_sem=s_fr.at[d, n],
                recv_sem=r_fr.at[d, n],
                device_id={"blk": me, "group": peer},
                device_id_type=MESH,
            )
            for n, (src, dst) in enumerate(((fresh_k, kwin), (fresh_v, vwin)))
        ]

    for d in range(1, ng):
        for c in quarter_copies(d):
            c.start()
    for d in range(1, ng):

        @pl.when(g + d < ng)
        def _():
            for c in fresh_copies(d):
                c.start()

    own = [
        pltpu.make_async_copy(src, dst.at[pl.ds(old_pages + g * mine, mine)], loc.at[n])
        for n, (src, dst) in enumerate(((fresh_k, kwin), (fresh_v, vwin)))
    ]
    for c in own:
        c.start()
    for i in range(mine):
        qbuf_k[g * mine + i] = fresh_k[i, g]
        qbuf_v[g * mine + i] = fresh_v[i, g]

    def wait_old(k, _):
        old_landed(k).wait_recv()
        return 0

    lax.fori_loop(1, nb, wait_old, 0)

    def pack(j, _):
        a = tab[1, j]
        comp_k[j] = recv_old[a, 0]
        comp_v[j] = recv_old[a, 1]
        return 0

    lax.fori_loop(0, old_pages, pack, 0)

    def window_copies(d, q):
        peer = lax.rem(g + d, ng)
        return [
            pltpu.make_async_remote_copy(
                src_ref=src.at[pl.ds(q * mine, mine)],
                dst_ref=dst.at[pl.ds(q * mine, mine), g],
                send_sem=s_ag.at[d, q, n],
                recv_sem=r_ag.at[d, q, n],
                device_id={"blk": me, "group": peer},
                device_id_type=MESH,
            )
            for n, (src, dst) in enumerate(((comp_k, kwin), (comp_v, vwin)))
        ]

    for q in range(ng):
        for d in range(1, ng):

            @pl.when(lax.rem(g + d, ng) <= q)
            def _():
                for c in window_copies(d, q):
                    c.start()

    own += [
        pltpu.make_async_copy(src, dst.at[pl.ds(0, old_pages), g], loc.at[2 + n])
        for n, (src, dst) in enumerate(((comp_k, kwin), (comp_v, vwin)))
    ]
    for c in own[2:]:
        c.start()

    def quarter_landed(d):
        peer = lax.rem(g + ng - d, ng)
        return [
            pltpu.make_async_remote_copy(
                src_ref=src.at[:, peer],
                dst_ref=dst.at[pl.ds(peer * mine, mine)],
                send_sem=s_q.at[d, n],
                recv_sem=r_q.at[d, n],
                device_id={"blk": me, "group": peer},
                device_id_type=MESH,
            )
            for n, (src, dst) in enumerate(((fresh_k, qbuf_k), (fresh_v, qbuf_v)))
        ]

    for d in range(1, ng):
        for c in quarter_landed(d):
            c.wait_recv()

    def fill_new(a, _):
        i = tab[2, a]
        send_new[a, 0] = qbuf_k[i]
        send_new[a, 1] = qbuf_v[i]
        return 0

    lax.fori_loop(0, nb, fill_new, 0)

    def new_copy(k):
        a = lax.rem(me + k, nb)
        return pltpu.make_async_remote_copy(
            src_ref=send_new.at[a],
            dst_ref=newrecv.at[me],
            send_sem=s_new.at[a],
            recv_sem=r_new.at[me],
            device_id={"blk": a, "group": g},
            device_id_type=MESH,
        )

    def new_landed(k):
        a = lax.rem(me + nb - k, nb)
        return pltpu.make_async_remote_copy(
            src_ref=send_new.at[a],
            dst_ref=newrecv.at[a],
            send_sem=s_new.at[a],
            recv_sem=r_new.at[a],
            device_id={"blk": a, "group": g},
            device_id_type=MESH,
        )

    def start_new(k, _):
        new_copy(k).start()
        return 0

    lax.fori_loop(1, nb, start_new, 0)
    own.append(pltpu.make_async_copy(send_new.at[me], newrecv.at[me], loc.at[4]))
    own[-1].start()

    def wait_sends(k, _):
        old_copy(k).wait_send()
        new_copy(k).wait_send()
        new_landed(k).wait_recv()
        return 0

    lax.fori_loop(1, nb, wait_sends, 0)
    for d in range(1, ng):
        for c in quarter_copies(d):
            c.wait_send()

        @pl.when(g + d < ng)
        def _():
            for c in fresh_copies(d):
                c.wait_send()

        @pl.when(g - d >= 0)
        def _():
            for c in fresh_copies(d):
                c.wait_recv()

    for q in range(ng):
        for d in range(1, ng):

            @pl.when(lax.rem(g + d, ng) <= q)
            def _():
                for c in window_copies(d, q):
                    c.wait_send()

            @pl.when(g <= q)
            def _():
                for c in window_copies(d, q):
                    c.wait_recv()

    for c in own:
        c.wait()


def attend_kernel(
    dims,
    tab,
    q_ref,
    cos_ref,
    sin_ref,
    kwin,
    vwin,
    w,
    kcache,
    vcache,
    newrecv,
    hidden,
    key_out,
    value_out,
    kbuf,
    vbuf,
    wbuf,
    qs,
    att,
    kpages,
    vpages,
    sem,
    page_sem,
    out_sem,
):
    nb, ng, tok, heads, hd, tile, scale, wchunk = dims
    g = lax.axis_index("group")
    win = kbuf.shape[0]
    keys = win - tok + tile
    half = hd // 2
    quarter = half // 2

    kv = [
        pltpu.make_async_copy(src.at[pl.ds(g * tok, win)], dst, sem.at[n])
        for n, (src, dst) in enumerate(((kwin, kbuf), (vwin, vbuf)))
    ]
    for c in kv:
        c.start()
    pool = [
        pltpu.make_async_copy(kcache, kpages, sem.at[2]),
        pltpu.make_async_copy(vcache, vpages, sem.at[3]),
    ]
    for c in pool:
        c.start()
    weight = pltpu.make_async_copy(w, wbuf, sem.at[4])
    weight.start()

    for t in range(tok // tile):
        rows = pl.ds(t * tile, tile)
        cosine, sine = cos_ref[rows, :], sin_ref[rows, :]
        for h in range(heads):
            lead = q_ref[rows, h * hd : h * hd + half].astype(jnp.float32)
            turned = pltpu.roll(lead, quarter, axis=1)
            roped = (lead * cosine + turned * sine).astype(jnp.bfloat16)
            qs[t, h * tile : (h + 1) * tile, :half] = roped * scale
            qs[t, h * tile : (h + 1) * tile, half:] = (
                q_ref[rows, h * hd + half : (h + 1) * hd] * scale
            )

    for c in pool:
        c.wait()

    def place(b, _):
        i = tab[3, b]

        @pl.when(i >= 0)
        def _():
            a = pltpu.make_async_copy(newrecv.at[b, 0], kpages.at[i], page_sem.at[b, 0])
            c = pltpu.make_async_copy(newrecv.at[b, 1], vpages.at[i], page_sem.at[b, 1])
            a.start()
            c.start()

        return 0

    lax.fori_loop(0, nb, place, 0)

    def placed(b, _):
        i = tab[3, b]

        @pl.when(i >= 0)
        def _():
            pltpu.make_async_copy(newrecv.at[b, 0], kpages.at[i], page_sem.at[b, 0]).wait()
            pltpu.make_async_copy(newrecv.at[b, 1], vpages.at[i], page_sem.at[b, 1]).wait()

        return 0

    for c in kv:
        c.wait()

    pair = 2 * tile
    first_fresh = win - tok - g * tok

    def run(with_old):
        def step(it, _):
            t = it // (heads // 2)
            hp = it % (heads // 2)
            q = qs[t, pl.ds(hp * pair, pair), :]
            start = pl.multiple_of(t * tile, tile)
            k = kbuf[pl.ds(start, keys), :]
            s = lax.dot_general(q, k, (((1,), (1,)), ((), ())), preferred_element_type=jnp.float32)
            r = lax.rem(lax.broadcasted_iota(jnp.int32, (pair, tile), 0), tile)
            c = lax.broadcasted_iota(jnp.int32, (pair, tile), 1)
            s = jnp.concatenate(
                [
                    jnp.where(c > r, s[:, :tile], NEG),
                    s[:, tile : keys - tile],
                    jnp.where(c <= r, s[:, keys - tile :], NEG),
                ],
                axis=1,
            )
            if not with_old:
                col = start + lax.broadcasted_iota(jnp.int32, (1, keys), 1)
                s = jnp.where(col >= first_fresh, s, NEG)
            m = jnp.max(s, axis=1, keepdims=True)
            p = jnp.exp(s - m)
            total = jnp.sum(p, axis=1, keepdims=True)
            o = jnp.dot(
                p.astype(jnp.bfloat16),
                vbuf[pl.ds(start, keys), :],
                preferred_element_type=jnp.float32,
            )
            o = (o / total).astype(jnp.bfloat16)
            rows = pl.ds(start, tile)
            col0 = pl.multiple_of(hp * 2 * hd, hd)
            att[rows, pl.ds(col0, hd)] = o[:tile]
            att[rows, pl.ds(pl.multiple_of(col0 + hd, hd), hd)] = o[tile:]
            return 0

        lax.fori_loop(0, (tok // tile) * (heads // 2), step, 0)

    length = tab[4, 0]

    @pl.when(length > 0)
    def _():
        run(True)

    @pl.when(length <= 0)
    def _():
        run(False)

    lax.fori_loop(0, nb, placed, 0)
    outs = [
        pltpu.make_async_copy(kpages, key_out, out_sem.at[0]),
        pltpu.make_async_copy(vpages, value_out, out_sem.at[1]),
    ]
    for c in outs:
        c.start()
    weight.wait()

    def project(n, _):
        cols = pl.ds(pl.multiple_of(n * wchunk, wchunk), wchunk)
        hidden[:, cols] = jnp.dot(
            att[...], wbuf[:, cols], preferred_element_type=jnp.float32
        ).astype(jnp.bfloat16)
        return 0

    lax.fori_loop(0, w.shape[1] // wchunk, project, 0)
    for c in outs:
        c.wait()


def body(queries, new_keys, new_values, key_cache, value_cache, out_weight, lengths, page_table):
    nb = lax.axis_size("blk")
    ng = lax.axis_size("group")
    me = lax.axis_index("blk")
    g = lax.axis_index("group")
    tok = queries.shape[1]
    hd = new_keys.shape[2]
    heads = queries.shape[2] // hd
    pages_here, rows = key_cache.shape[:2]
    slots = page_table.shape[1]
    group_len = tok * ng
    fresh = group_len // (rows * ng)
    old = slots - fresh
    mine = fresh // ng
    bf16 = jnp.bfloat16

    length = lengths[me]
    positions = length + g * tok + jnp.arange(tok, dtype=jnp.int32)
    cosine, sine = rope_tables(positions, hd // 4)
    half = hd // 2
    lead = new_keys[0, :, :half].astype(jnp.float32)
    turned = jnp.concatenate([lead[:, half // 2 :], lead[:, : half // 2]], axis=1)
    roped = jnp.concatenate(
        [(lead * cosine + turned * sine).astype(bf16), new_keys[0, :, half:]], axis=1
    )

    owner = page_table // pages_here
    local = page_table % pages_here
    here = owner == me
    my_owner = owner[me]
    ids = jnp.arange(nb, dtype=jnp.int32)
    wanted = jnp.sum(jnp.where(here[:, :old], local[:, :old], 0), axis=1)
    target = jnp.sum(jnp.where(here[:, old:], local[:, old:] + 1, 0), axis=1) - 1
    source = jnp.sum(
        jnp.where(
            my_owner[None, old:] == ids[:, None], jnp.arange(fresh, dtype=jnp.int32)[None, :], 0
        ),
        axis=1,
    )
    tab = jnp.stack(
        [wanted, jnp.pad(my_owner[:old], (0, nb - old)), source, target, jnp.full((nb,), length)]
    ).astype(jnp.int32)

    shape4 = (mine, ng, rows, hd)
    kwin, vwin, newrecv = pl.pallas_call(
        functools.partial(comm_kernel, (nb, ng, old, mine)),
        out_shape=(
            jax.ShapeDtypeStruct((old + fresh, ng, rows, hd), bf16),
            jax.ShapeDtypeStruct((old + fresh, ng, rows, hd), bf16),
            jax.ShapeDtypeStruct((nb, 2, rows, hd), bf16),
        ),
        in_specs=[SM, VM, VM, VM, VM],
        out_specs=(ANY, ANY, ANY),
        scratch_shapes=[
            pltpu.VMEM((nb, 2, rows, hd), bf16),
            pltpu.VMEM((nb, 2, rows, hd), bf16),
            pltpu.VMEM((old, rows, hd), bf16),
            pltpu.VMEM((old, rows, hd), bf16),
            pltpu.VMEM((fresh, rows, hd), bf16),
            pltpu.VMEM((fresh, rows, hd), bf16),
            pltpu.VMEM((nb, 2, rows, hd), bf16),
            pltpu.SemaphoreType.DMA((nb,)),
            pltpu.SemaphoreType.DMA((nb,)),
            pltpu.SemaphoreType.DMA((ng, 2)),
            pltpu.SemaphoreType.DMA((ng, 2)),
            pltpu.SemaphoreType.DMA((ng, 2)),
            pltpu.SemaphoreType.DMA((ng, 2)),
            pltpu.SemaphoreType.DMA((ng, ng, 2)),
            pltpu.SemaphoreType.DMA((ng, ng, 2)),
            pltpu.SemaphoreType.DMA((nb,)),
            pltpu.SemaphoreType.DMA((nb,)),
            pltpu.SemaphoreType.DMA((5,)),
        ],
        compiler_params=pltpu.CompilerParams(collective_id=0, has_side_effects=True),
        name="exchange",
    )(tab, roped.reshape(shape4), new_values[0].reshape(shape4), key_cache, value_cache)

    tile = rows * ng
    win = old * tile + tok
    d_out = out_weight.shape[1]
    hidden, key_out, value_out = pl.pallas_call(
        functools.partial(attend_kernel, (nb, ng, tok, heads, hd, tile, hd**-0.5, 512)),
        out_shape=(
            jax.ShapeDtypeStruct((tok, d_out), bf16),
            jax.ShapeDtypeStruct(key_cache.shape, bf16),
            jax.ShapeDtypeStruct(value_cache.shape, bf16),
        ),
        in_specs=[SM, VM, VM, VM, ANY, ANY, ANY, ANY, ANY, ANY],
        out_specs=(VM, ANY, ANY),
        scratch_shapes=[
            pltpu.VMEM((win, hd), bf16),
            pltpu.VMEM((win, hd), bf16),
            pltpu.VMEM(out_weight.shape, bf16),
            pltpu.VMEM((tok // tile, heads * tile, hd), bf16),
            pltpu.VMEM((tok, heads * hd), bf16),
            pltpu.VMEM(key_cache.shape, bf16),
            pltpu.VMEM(value_cache.shape, bf16),
            pltpu.SemaphoreType.DMA((5,)),
            pltpu.SemaphoreType.DMA((nb, 2)),
            pltpu.SemaphoreType.DMA((2,)),
        ],
        compiler_params=pltpu.CompilerParams(vmem_limit_bytes=60 << 20),
        name="attend",
    )(
        tab,
        queries[0],
        cosine,
        sine,
        kwin.reshape(-1, hd),
        vwin.reshape(-1, hd),
        out_weight,
        key_cache,
        value_cache,
        newrecv,
    )
    return (hidden[None], key_out, value_out)


def solution(mesh):
    split = P("blk", "group", None)
    return jax.shard_map(
        body,
        mesh=mesh,
        in_specs=(split, split, split, split, split, P(), P(), P()),
        out_specs=(split, split, split),
        check_vma=False,
    )
```

time: 1180 us -> 134 us (0.11)
  waiting for transfers between devices: 894 us -> 0 us
  matrix products: 142 us -> 0 us
  Pallas kernels: 0 us -> 121 us
  local copies, waits for them, and re-layouts: 51.9 us -> 2.71 us
  other arithmetic: 52.3 us -> 6.83 us
  starting transfers between devices: 20.8 us -> 0 us
  between operations: 15.4 us -> 1.37 us
    all_gather x6 -> x0, waiting for transfers between devices: 893 us -> none  [the longest x1 444 us: body(): lax.all_gather(value_cache, 'blk', axis=0, tiled=True)]
    dot_general x19 -> x0, matrix products: 142 us -> none  [the longest x8 78.7 us: attend_block(): jnp.einsum('thk,kd->thd', weights.astype(jnp.bfloat16), value_rows, prefe...]
    pallas_call x0 -> x2, Pallas kernels: none -> 121 us  [the longest x1 71.6 us: body(): pl.pallas_call(functools.partial(comm_kernel, (nb, ng, old, mine)), out_s...]
    reduce_sum x10 -> x2, other arithmetic: 33.6 us -> 0.29 us  [the longest x1 0.18 us: body(): jnp.sum(jnp.where(here[:, old:], local[:, old:] + 1, 0), axis=1) - 1]
    all_to_all x2 -> x0, starting transfers between devices: 20.3 us -> none  [the longest x1 10.4 us: body(): lax.all_to_all(send_new_values, 'blk', split_axis=0, concat_axis=0, tiled...]
    gather x2 -> x0, local copies, waits for them, and re-layouts: 15 us -> none  [the longest x1 7.52 us: body(): old_keys = jnp.where(inside[:, None, None], pieces[0][clipped], blank_pages)]
    unnamed x94 -> x0, local copies, waits for them, and re-layouts: 13.5 us -> none
  transfers between devices with their start and end apart: 8 -> 0, of which waited for: 3 -> 0; matrix products, arithmetic and copies ran while one was open for 9% -> 0% of each run, Pallas kernels for 0% -> 0%
where the time goes in v1:
time: 134 us; the launch traced here: 132 us
  Pallas kernels  121 us (90%)
  other arithmetic  6.83 us (5%)
  local copies, waits for them, and re-layouts  2.71 us (2%)
  between operations  1.37 us (1%)
    pallas_call x1, Pallas kernels, body(): pl.pallas_call(functools.partial(comm_kernel, (nb, ng, old, mine)), out_s...  71.6 us
    pallas_call x1, Pallas kernels, body(): pl.pallas_call(functools.partial(attend_kernel, (nb, ng, tok, heads, hd,...  49.1 us

profile of v1, /device:TPU:1, one launch (start us, length us, event | category | flops | bytes accessed | tf_op | source)
XLA Modules:
  0.0 131.6 jit_solution(1474695481890021799)
XLA Ops:
  0.6 1.2 dynamic_slice.7
  2.5 0.6 stack_broadcast_in_dim.3
  3.2 0.7 add_select_fusion
  4.0 0.7 broadcast_compare_fusion
  4.7 0.2 fusion.6
  4.9 0.1 slice_bitcast_fusion
  5.0 0.1 select_reduce_fusion
  5.1 0.6 stack.16.tab
  5.7 1.0 fusion.4
  6.7 0.1 fusion.9
  6.9 1.0 fusion.3
  7.9 0.3 fusion.1
  8.1 0.7 pad_maximum_fusion.2.fresh_k
  8.9 1.0 fusion.2
  9.9 1.0 pad_maximum_fusion
  10.9 71.6 %exchange.1 = (bf16[32,4,32,256]{3,2,1,0:T(8,128)(2,1)}, bf16[32,4,32,256]{3,2,1,0:T(8,128)(2,1)}, bf16[32,2,32,256]{3,2,1,0:T(8,128)(2,1)}) custom-call(s32[5,32]{1,0:T(8,128)} %stack.16.tab, bf16[4,4,32,256]{3,2,1,0:T(8,128)(2,1)} %pad_maximum_fusion.2.fresh_k, bf16[4,4,32,256]{3,2,1,0:T(8,128)(2,1)} %bitcast.29, bf16[40,32,256]{2,1,0:T(8,128)(2,1)} %kcache.3, ...), custom_call_target="tpu_custom_call" | custom-call | tf_op jit(solution)/shard_map/exchange/pallas_call | solution.py:503
  82.5 49.1 %attend.1 = (bf16[512,2560]{1,0:T(8,128)(2,1)}, bf16[40,32,256]{2,1,0:T(8,128)(2,1)}, bf16[40,32,256]{2,1,0:T(8,128)(2,1)}) custom-call(s32[5,32]{1,0:T(8,128)} %stack.16.tab, bf16[512,2560]{1,0:T(8,128)(2,1)} %bitcast.22, f32[512,128]{1,0:T(8,128)} %get-tuple-element.34.cos_ref, f32[512,128]{1,0:T(8,128)} %get-tuple-element.35.sin_ref, ...), custom_call_target="tpu_custom_call" | custom-call | tf_op jit(solution)/shard_map/attend/pallas_call | solution.py:539
  (5 shorter events, 0.0 us)

commit v2 on v0

v2 whole, which is shorter than its diff:
```python
import functools

import jax
import jax.numpy as jnp
from jax import lax
from jax.experimental import pallas as pl
from jax.experimental.pallas import tpu as pltpu
from jax.sharding import PartitionSpec as P

MESH = pl.DeviceIdType.MESH
NEG = -1e30
ANY = pl.BlockSpec(memory_space=pl.ANY)
VM = pl.BlockSpec(memory_space=pltpu.VMEM)
SM = pl.BlockSpec(memory_space=pltpu.SMEM)


def rope_tables(positions, quarter):
    freq_table = 10000.0 ** (-jnp.arange(quarter, dtype=jnp.float32) / quarter)
    angles = positions.astype(jnp.float32)[..., None] * freq_table
    cosine, sine = jnp.cos(angles), jnp.sin(angles)
    return (
        jnp.concatenate([cosine, cosine], axis=-1),
        jnp.concatenate([-sine, sine], axis=-1),
    )


def layer_kernel(
    dims,
    tab,
    queries,
    fresh_k,
    fresh_v,
    kcache,
    vcache,
    cos_ref,
    sin_ref,
    attended,
    newrecv,
    q_ref,
    qs,
    att,
    kbuf,
    vbuf,
    send_old,
    recv_k,
    recv_v,
    comp,
    qbuf,
    send_new,
    score0,
    score1,
    s_old,
    r_old,
    s_fr,
    r_fr,
    s_q,
    r_q,
    s_ag,
    r_ag,
    s_new,
    r_new,
    loc,
    out_sem,
):
    nb, ng, old_pages, mine, heads, hd, scale = dims
    me = lax.axis_index("blk")
    g = lax.axis_index("group")
    core = lax.rem(g, 2)
    hi = g // 2
    partner = 2 * hi + 1 - core
    across = 2 * (1 - hi) + core
    other = 2 * (1 - hi)
    windows = (kbuf, vbuf)
    fresh = (fresh_k, fresh_v)
    caches = (kcache, vcache)
    recv_old = (recv_k, recv_v)
    rows = kcache.shape[1]
    tile = rows * ng
    half = hd // 2
    quarter = half // 2

    def remote(src, dst, ssem, rsem, blk, grp):
        return pltpu.make_async_remote_copy(
            src_ref=src,
            dst_ref=dst,
            send_sem=ssem,
            recv_sem=rsem,
            device_id={"blk": blk, "group": grp},
            device_id_type=MESH,
        )

    get_q = pltpu.make_async_copy(queries, q_ref, loc.at[0])
    get_q.start()

    barrier = pltpu.get_barrier_semaphore()

    def greet(k, _):
        pl.semaphore_signal(
            barrier, inc=1, device_id={"blk": lax.rem(me + k, nb), "group": g}, device_id_type=MESH
        )
        return 0

    lax.fori_loop(1, nb, greet, 0)
    for d in range(1, ng):
        pl.semaphore_signal(
            barrier, inc=1, device_id={"blk": me, "group": lax.rem(g + d, ng)}, device_id_type=MESH
        )

    for n in range(2):

        def fill(a, _):
            send_old[n, a] = caches[n][tab[0, a]]
            return 0

        lax.fori_loop(0, nb, fill, 0)
        recv_old[n][me] = send_old[n, me]
    pl.semaphore_wait(barrier, nb - 1 + ng - 1)

    def old_copy(n, k):
        a = lax.rem(me + k, nb)
        return remote(
            send_old.at[n, a], recv_old[n].at[me], s_old.at[n, a], r_old.at[n, me], a, g
        )

    def old_landed(n, k):
        a = lax.rem(me + nb - k, nb)
        return remote(send_old.at[n, a], recv_old[n].at[a], s_old.at[n, a], r_old.at[n, a], a, g)

    for n in range(2):

        def start_old(k, _):
            old_copy(n, k).start()
            return 0

        lax.fori_loop(1, nb, start_old, 0)

    def fresh_at(src, dst):
        return pl.ds(old_pages + mine * (src - dst), mine)

    def fresh_near(n):
        return remote(
            fresh[n], windows[n].at[fresh_at(g, partner)], s_fr.at[n, 0], r_fr.at[n, g], me, partner
        )

    def fresh_far(n):
        return remote(
            fresh[n], windows[n].at[fresh_at(g, across)], s_fr.at[n, 1], r_fr.at[n, g], me, across
        )

    def fresh_pass(n):
        return remote(
            windows[n].at[fresh_at(across, g)],
            windows[n].at[fresh_at(across, partner)],
            s_fr.at[n, 2],
            r_fr.at[n, across],
            me,
            partner,
        )

    def fresh_from(n, src):
        return remote(
            fresh[n], windows[n].at[fresh_at(src, g)], s_fr.at[n, 0], r_fr.at[n, src], me, partner
        )

    def quarter_to(n, dst):
        return remote(
            fresh[n].at[:, dst],
            qbuf.at[n, pl.ds(mine * g, mine)],
            s_q.at[n, dst],
            r_q.at[n, g],
            me,
            dst,
        )

    def quarter_from(n, src):
        return remote(
            fresh[n].at[:, g],
            qbuf.at[n, pl.ds(mine * src, mine)],
            s_q.at[n, g],
            r_q.at[n, src],
            me,
            partner,
        )

    @pl.when(hi == 0)
    def _():
        for n in range(2):
            fresh_far(n).start()

    @pl.when(core == 0)
    def _():
        for n in range(2):
            fresh_near(n).start()

    for d in range(ng - 1):

        @pl.when(g > d)
        def _():
            for n in range(2):
                quarter_to(n, d).start()

    for n in range(2):
        windows[n][pl.ds(old_pages, mine)] = fresh[n][...]
        qbuf[n, pl.ds(mine * g, mine)] = fresh[n][:, g]

    get_q.wait()
    tiles = q_ref.shape[0] // tile
    for t in range(tiles):
        trows = pl.ds(t * tile, tile)
        cosine, sine = cos_ref[trows, :], sin_ref[trows, :]
        for h in range(heads):
            lead = q_ref[trows, h * hd : h * hd + half].astype(jnp.float32)
            turned = pltpu.roll(lead, quarter, axis=1)
            roped = (lead * cosine + turned * sine).astype(jnp.bfloat16)
            qs[t, h * tile : (h + 1) * tile, :half] = roped * scale
            qs[t, h * tile : (h + 1) * tile, half:] = (
                q_ref[trows, h * hd + half : (h + 1) * hd] * scale
            )

    def block(q, dst):
        return pl.ds(mine * (q - dst), mine)

    def ag_near(n, q):
        return remote(
            comp.at[n, pl.ds(mine * q, mine)],
            windows[n].at[block(q, partner), g],
            s_ag.at[n, q, 0],
            r_ag.at[n, q, g],
            me,
            partner,
        )

    def ag_far(n, q, dst):
        return remote(
            comp.at[n, pl.ds(mine * q, mine)],
            windows[n].at[block(q, dst), g],
            s_ag.at[n, q, 1],
            r_ag.at[n, q, g],
            me,
            dst,
        )

    def ag_pass(n, q):
        return remote(
            windows[n].at[block(q, g), across],
            windows[n].at[block(q, partner), across],
            s_ag.at[n, q, 2],
            r_ag.at[n, q, across],
            me,
            partner,
        )

    def ag_from(n, q, src):
        return remote(
            comp.at[n, pl.ds(mine * q, mine)],
            windows[n].at[block(q, g), src],
            s_ag.at[n, q, 0],
            r_ag.at[n, q, src],
            me,
            partner,
        )

    def far_do(n, q, act):
        @pl.when(other + 1 <= q)
        def _():
            act(ag_far(n, q, across))

        @pl.when(other == q)
        def _():
            act(ag_far(n, q, other))

    def start(c):
        c.start()

    def sent(c):
        c.wait_send()

    for n in range(2):

        def wait_old(k, _):
            old_landed(n, k).wait_recv()
            return 0

        lax.fori_loop(1, nb, wait_old, 0)

        def pack(j, _):
            comp[n, j] = recv_old[n][tab[1, j]]
            return 0

        lax.fori_loop(0, old_pages, pack, 0)
        for q in range(ng):
            far_do(n, q, start)

            @pl.when(partner <= q)
            def _():
                ag_near(n, q).start()

            @pl.when(g <= q)
            def _():
                windows[n][block(q, g), g] = comp[n, pl.ds(mine * q, mine)]

        if n == 0:

            @pl.when(hi == 1)
            def _():
                for m in range(2):
                    fresh_from(m, across).wait_recv()
                    fresh_pass(m).start()

    @pl.when(core == 1)
    def _():
        for n in range(2):
            fresh_from(n, partner).wait_recv()

    @pl.when(hi == 1)
    def _():
        for n in range(2):
            fresh_from(n, 1 - core).wait_recv()

    for src in range(ng):

        @pl.when(src < g)
        def _():
            for n in range(2):
                qbuf[n, pl.ds(mine * src, mine)] = windows[n][fresh_at(src, g), g]

        @pl.when(src > g)
        def _():
            for n in range(2):
                quarter_from(n, src).wait_recv()

    def fill_new(a, _):
        i = tab[2, a]
        send_new[a, 0] = qbuf[0, i]
        send_new[a, 1] = qbuf[1, i]
        return 0

    lax.fori_loop(0, nb, fill_new, 0)

    def new_copy(k):
        a = lax.rem(me + k, nb)
        return remote(send_new.at[a], newrecv.at[me], s_new.at[a], r_new.at[me], a, g)

    def new_landed(k):
        a = lax.rem(me + nb - k, nb)
        return remote(send_new.at[a], newrecv.at[a], s_new.at[a], r_new.at[a], a, g)

    def start_new(k, _):
        new_copy(k).start()
        return 0

    lax.fori_loop(1, nb, start_new, 0)
    keep = pltpu.make_async_copy(send_new.at[me], newrecv.at[me], loc.at[1])
    keep.start()

    for n in range(2):
        for q in range(ng):

            @pl.when(2 * hi + 1 <= q)
            def _():
                ag_from(n, q, across).wait_recv()
                ag_pass(n, q).start()

    for n in range(2):
        for q in range(ng):

            @pl.when(g <= q)
            def _():
                ag_from(n, q, partner).wait_recv()
                ag_from(n, q, other + 1 - core).wait_recv()

            @pl.when(2 * hi == q)
            def _():
                @pl.when(core == 0)
                def _():
                    ag_from(n, q, across).wait_recv()

    parts = 2
    group = heads // parts
    high = group * tile
    total_parts = tiles * parts
    pages = old_pages + 1
    keys = pages * tile
    empty = tab[4, 0] <= 0

    def scores(it, dst):
        t = it // parts
        first = pl.multiple_of(lax.rem(it, parts) * high, high)
        k = kbuf[pl.ds(t, pages)].reshape(keys, hd)
        dst[...] = lax.dot_general(
            qs[t, pl.ds(first, high), :],
            k,
            (((1,), (1,)), ((), ())),
            preferred_element_type=jnp.float32,
        )

    def softmax(it, src):
        t = it // parts
        part = lax.rem(it, parts)
        r = lax.rem(lax.broadcasted_iota(jnp.int32, (high, tile), 0), tile)
        c = lax.broadcasted_iota(jnp.int32, (high, tile), 1)
        s = jnp.concatenate(
            [
                jnp.where(c > r, src[:, :tile], NEG),
                src[:, tile : keys - tile],
                jnp.where(c <= r, src[:, keys - tile :], NEG),
            ],
            axis=1,
        )
        col = (t + mine * g) * tile + lax.broadcasted_iota(jnp.int32, (1, keys), 1)
        hidden_key = jnp.logical_and(col < old_pages * tile, empty)
        s = jnp.where(hidden_key, NEG, s)
        m = jnp.max(s, axis=1, keepdims=True)
        p = jnp.exp(s - m)
        total = jnp.sum(p, axis=1, keepdims=True)
        o = jnp.dot(
            p.astype(jnp.bfloat16),
            vbuf[pl.ds(t, pages)].reshape(keys, hd),
            preferred_element_type=jnp.float32,
        )
        o = (o / total).astype(jnp.bfloat16)
        at = pl.ds(pl.multiple_of(t * tile, tile), tile)
        for h in range(group):
            cols = pl.ds(pl.multiple_of((part * group + h) * hd, hd), hd)
            att[at, cols] = o[h * tile : (h + 1) * tile]

    scores(0, score0)

    def step(i, _):
        scores(2 * i + 1, score1)
        softmax(2 * i, score0)
        scores(lax.rem(2 * i + 2, total_parts), score0)
        softmax(2 * i + 1, score1)
        return 0

    lax.fori_loop(0, total_parts // 2, step, 0)
    put = pltpu.make_async_copy(att, attended, out_sem.at[0])
    put.start()

    def wait_rest(k, _):
        old_copy(0, k).wait_send()
        old_copy(1, k).wait_send()
        new_copy(k).wait_send()
        new_landed(k).wait_recv()
        return 0

    lax.fori_loop(1, nb, wait_rest, 0)
    keep.wait()

    @pl.when(hi == 0)
    def _():
        for n in range(2):
            fresh_far(n).wait_send()

    @pl.when(core == 0)
    def _():
        for n in range(2):
            fresh_near(n).wait_send()

    @pl.when(hi == 1)
    def _():
        for n in range(2):
            fresh_pass(n).wait_send()

    for n in range(2):
        for d in range(ng - 1):

            @pl.when(g > d)
            def _():
                quarter_to(n, d).wait_send()

        for q in range(ng):
            far_do(n, q, sent)

            @pl.when(partner <= q)
            def _():
                ag_near(n, q).wait_send()

            @pl.when(2 * hi + 1 <= q)
            def _():
                ag_pass(n, q).wait_send()

    put.wait()


def project_kernel(
    nb, tab, att, w, kcache, vcache, newrecv, hidden, key_out, value_out, pages, sem, page_sem
):
    n = pl.program_id(0)
    caches = (kcache, vcache)
    outs = (key_out, value_out)

    @pl.when(n == 0)
    def _():
        for i in range(2):
            pltpu.make_async_copy(caches[i], pages.at[i], sem.at[i]).start()

    def place(b, act):
        i = tab[3, b]

        @pl.when(i >= 0)
        def _():
            for m in range(2):
                act(
                    pltpu.make_async_copy(newrecv.at[b, m], pages.at[m, i], page_sem.at[b, m])
                )

    @pl.when(n == 1)
    def _():
        for i in range(2):
            pltpu.make_async_copy(caches[i], pages.at[i], sem.at[i]).wait()

        def go(b, _):
            place(b, lambda c: c.start())
            return 0

        lax.fori_loop(0, nb, go, 0)

    @pl.when(n == 2)
    def _():
        def done(b, _):
            place(b, lambda c: c.wait())
            return 0

        lax.fori_loop(0, nb, done, 0)
        for i in range(2):
            pltpu.make_async_copy(pages.at[i], outs[i], sem.at[2 + i]).start()

    hidden[...] = jnp.dot(att[...], w[...], preferred_element_type=jnp.float32).astype(
        jnp.bfloat16
    )

    @pl.when(n == pl.num_programs(0) - 1)
    def _():
        for i in range(2):
            pltpu.make_async_copy(pages.at[i], outs[i], sem.at[2 + i]).wait()


def body(queries, new_keys, new_values, key_cache, value_cache, out_weight, lengths, page_table):
    nb = lax.axis_size("blk")
    ng = lax.axis_size("group")
    me = lax.axis_index("blk")
    g = lax.axis_index("group")
    tok = queries.shape[1]
    hd = new_keys.shape[2]
    heads = queries.shape[2] // hd
    pages_here, rows = key_cache.shape[:2]
    slots = page_table.shape[1]
    group_len = tok * ng
    fresh = group_len // (rows * ng)
    old = slots - fresh
    mine = fresh // ng
    bf16 = jnp.bfloat16

    length = lengths[me]
    positions = length + g * tok + jnp.arange(tok, dtype=jnp.int32)
    cosine, sine = rope_tables(positions, hd // 4)
    half = hd // 2
    lead = new_keys[0, :, :half].astype(jnp.float32)
    turned = jnp.concatenate([lead[:, half // 2 :], lead[:, : half // 2]], axis=1)
    roped = jnp.concatenate(
        [(lead * cosine + turned * sine).astype(bf16), new_keys[0, :, half:]], axis=1
    )

    owner = page_table // pages_here
    local = page_table % pages_here
    here = owner == me
    my_owner = owner[me]
    ids = jnp.arange(nb, dtype=jnp.int32)
    wanted = jnp.sum(jnp.where(here[:, :old], local[:, :old], 0), axis=1)
    target = jnp.sum(jnp.where(here[:, old:], local[:, old:] + 1, 0), axis=1) - 1
    source = jnp.sum(
        jnp.where(
            my_owner[None, old:] == ids[:, None], jnp.arange(fresh, dtype=jnp.int32)[None, :], 0
        ),
        axis=1,
    )
    tab = jnp.stack(
        [wanted, jnp.pad(my_owner[:old], (0, nb - old)), source, target, jnp.full((nb,), length)]
    ).astype(jnp.int32)

    shape4 = (mine, ng, rows, hd)
    tile = rows * ng
    keys = (old + 1) * tile
    dma = pltpu.SemaphoreType.DMA
    attended, newrecv = pl.pallas_call(
        functools.partial(layer_kernel, (nb, ng, old, mine, heads, hd, hd**-0.5)),
        out_shape=(
            jax.ShapeDtypeStruct((tok, heads * hd), bf16),
            jax.ShapeDtypeStruct((nb, 2, rows, hd), bf16),
        ),
        in_specs=[SM, ANY, VM, VM, VM, VM, VM, VM],
        out_specs=(ANY, ANY),
        scratch_shapes=[
            pltpu.VMEM((tok, heads * hd), bf16),
            pltpu.VMEM((tok // tile, heads * tile, hd), bf16),
            pltpu.VMEM((tok, heads * hd), bf16),
            pltpu.VMEM((old + mine, ng, rows, hd), bf16),
            pltpu.VMEM((old + mine, ng, rows, hd), bf16),
            pltpu.VMEM((2, nb, rows, hd), bf16),
            pltpu.VMEM((nb, rows, hd), bf16),
            pltpu.VMEM((nb, rows, hd), bf16),
            pltpu.VMEM((2, old, rows, hd), bf16),
            pltpu.VMEM((2, fresh, rows, hd), bf16),
            pltpu.VMEM((nb, 2, rows, hd), bf16),
            pltpu.VMEM((heads // 2 * tile, keys), jnp.float32),
            pltpu.VMEM((heads // 2 * tile, keys), jnp.float32),
            dma((2, nb)),
            dma((2, nb)),
            dma((2, 3)),
            dma((2, ng)),
            dma((2, ng)),
            dma((2, ng)),
            dma((2, ng, 3)),
            dma((2, ng, ng)),
            dma((nb,)),
            dma((nb,)),
            dma((2,)),
            dma((1,)),
        ],
        compiler_params=pltpu.CompilerParams(
            collective_id=0, has_side_effects=True, vmem_limit_bytes=60 << 20
        ),
        name="layer",
    )(
        tab,
        queries[0],
        roped.reshape(shape4),
        new_values[0].reshape(shape4),
        key_cache,
        value_cache,
        cosine,
        sine,
    )

    d_out = out_weight.shape[1]
    chunk = d_out // 5
    hidden, key_out, value_out = pl.pallas_call(
        functools.partial(project_kernel, nb),
        grid=(d_out // chunk,),
        out_shape=(
            jax.ShapeDtypeStruct((tok, d_out), bf16),
            jax.ShapeDtypeStruct(key_cache.shape, bf16),
            jax.ShapeDtypeStruct(value_cache.shape, bf16),
        ),
        in_specs=[
            SM,
            pl.BlockSpec((tok, heads * hd), lambda n: (0, 0)),
            pl.BlockSpec((heads * hd, chunk), lambda n: (0, n)),
            ANY,
            ANY,
            ANY,
        ],
        out_specs=(pl.BlockSpec((tok, chunk), lambda n: (0, n)), ANY, ANY),
        scratch_shapes=[
            pltpu.VMEM((2, *key_cache.shape), bf16),
            dma((4,)),
            dma((nb, 2)),
        ],
        compiler_params=pltpu.CompilerParams(vmem_limit_bytes=60 << 20),
        name="project",
    )(tab, attended, out_weight, key_cache, value_cache, newrecv)
    return (hidden[None], key_out, value_out)


def solution(mesh):
    split = P("blk", "group", None)
    return jax.shard_map(
        body,
        mesh=mesh,
        in_specs=(split, split, split, split, split, P(), P(), P()),
        out_specs=(split, split, split),
        check_vma=False,
    )
```

time: 1180 us -> 109 us (0.09)
  the two profiles are of different devices: /device:TPU:1 before, /device:TPU:75 now
where the time goes in v2:
time: 109 us
  Pallas kernels  97.8 us (90%)
  other arithmetic  6.8 us (6%)
  local copies, waits for them, and re-layouts  2.71 us (2%)
  between operations  1.53 us (1%)
    pallas_call x1, Pallas kernels, body(): pl.pallas_call(functools.partial(layer_kernel, (nb, ng, old, mine, heads,...  84.8 us
    pallas_call x1, Pallas kernels, body(): pl.pallas_call(functools.partial(project_kernel, nb), grid=(d_out // chun...  13 us

profile of v2, /device:TPU:75, one launch (start us, length us, event | category | flops | bytes accessed | tf_op | source)
XLA Modules:
  0.0 108.9 jit_solution(9185441131526445541)
XLA Ops:
  0.6 1.2 %dynamic_slice.7 = s32[1]{0:T(128)} dynamic-slice(s32[32]{0:T(128)} %param.14, s32[]{:T(128)S(6)} %select_n.30), dynamic_slice_sizes={1} | dynamic-slice | bytes 12 | tf_op jit(solution)/shard_map/dynamic_slice | solution.py:555
  2.5 0.6 stack_broadcast_in_dim.3
  3.2 0.7 add_select_fusion
  4.0 0.7 broadcast_compare_fusion
  4.7 0.2 fusion.6
  4.9 0.1 slice_bitcast_fusion
  5.0 0.1 select_reduce_fusion
  5.1 0.6 stack.16.tab
  5.7 1.0 fusion.4
  6.7 0.1 fusion.9
  6.9 1.0 fusion.3
  7.9 0.3 fusion.1
  8.1 0.7 pad_maximum_fusion.fresh_k
  8.9 1.0 fusion.2
  9.9 1.0 pad_maximum_fusion.1
  10.9 84.8 %layer.1 = (bf16[512,2560]{1,0:T(8,128)(2,1)}, bf16[32,2,32,256]{3,2,1,0:T(8,128)(2,1)}) custom-call(s32[5,32]{1,0:T(8,128)} %stack.16.tab, bf16[512,2560]{1,0:T(8,128)(2,1)} %bitcast.20, bf16[4,4,32,256]{3,2,1,0:T(8,128)(2,1)} %pad_maximum_fusion.fresh_k, bf16[4,4,32,256]{3,2,1,0:T(8,128)(2,1)} %bitcast.25, bf16[40,32,256]{2,1,0:T(8,128)(2,1)} %kcache.3, ...), custom_call_target="tpu_custom_call" | custom-call | tf_op jit(solution)/shard_map/layer/pallas_call | solution.py:586
  95.7 13.0 %project.1 = (bf16[512,2560]{1,0:T(8,128)(2,1)}, bf16[40,32,256]{2,1,0:T(8,128)(2,1)}, bf16[40,32,256]{2,1,0:T(8,128)(2,1)}) custom-call(s32[5,32]{1,0:T(8,128)} %stack.16.tab, bf16[512,2560]{1,0:T(8,128)(2,1)} %get-tuple-element.8.att, bf16[2560,2560]{1,0:T(8,128)(2,1)} %w.1, bf16[40,32,256]{2,1,0:T(8,128)(2,1)} %kcache.3, bf16[40,32,256]{2,1,0:T(8,128)(2,1)} %vcache.3, ...), custom_call_target="tpu_custom_call" | custom-call | tf_op jit(solution)/shard_map/project/pallas_call | solution.py:638
  (5 shorter events, 0.0 us)

commit v3 on v2

v3 whole, which is shorter than its diff:
```python
import functools

import jax
import jax.numpy as jnp
from jax import lax
from jax.experimental import pallas as pl
from jax.experimental.pallas import tpu as pltpu
from jax.sharding import PartitionSpec as P

MESH = pl.DeviceIdType.MESH
NEG = -1e30
ANY = pl.BlockSpec(memory_space=pl.ANY)
VM = pl.BlockSpec(memory_space=pltpu.VMEM)
SM = pl.BlockSpec(memory_space=pltpu.SMEM)


def layer_kernel(
    dims,
    tab,
    table,
    lengths,
    freq,
    new_k,
    fresh_v,
    kcache,
    vcache,
    queries,
    weight,
    hidden,
    key_out,
    value_out,
    fresh_k,
    cos_ref,
    sin_ref,
    q_ref,
    wbuf,
    qs,
    hid,
    pages,
    newrecv,
    kbuf,
    vbuf,
    send_old,
    recv_k,
    recv_v,
    comp,
    qbuf,
    send_new,
    score0,
    score1,
    prob0,
    prob1,
    sums0,
    sums1,
    s_old,
    r_old,
    s_fr,
    r_fr,
    s_q,
    r_q,
    s_ag,
    r_ag,
    s_new,
    r_new,
    loc,
    out_sem,
    w_sem,
):
    nb, ng, old_pages, mine, heads, hd, scale = dims
    pages_here = kcache.shape[0]
    me = lax.axis_index("blk")
    g = lax.axis_index("group")
    core = lax.rem(g, 2)
    hi = g // 2
    partner = 2 * hi + 1 - core
    across = 2 * (1 - hi) + core
    other = 2 * (1 - hi)
    windows = (kbuf, vbuf)
    fresh = (fresh_k, fresh_v)
    caches = (kcache, vcache)
    recv_old = (recv_k, recv_v)
    rows = kcache.shape[1]
    tile = rows * ng
    half = hd // 2
    quarter = half // 2

    def remote(src, dst, ssem, rsem, blk, grp):
        return pltpu.make_async_remote_copy(
            src_ref=src,
            dst_ref=dst,
            send_sem=ssem,
            recv_sem=rsem,
            device_id={"blk": blk, "group": grp},
            device_id_type=MESH,
        )

    get_q = pltpu.make_async_copy(queries, q_ref, loc.at[0])
    get_q.start()
    chunks = 5
    slots = wbuf.shape[0]
    wide = wbuf.shape[2]

    def get_w(n):
        cols = pl.ds(pl.multiple_of(n * wide, wide), wide)
        return pltpu.make_async_copy(
            weight.at[:, cols], wbuf.at[lax.rem(n, slots)], w_sem.at[lax.rem(n, slots)]
        )

    for n in range(slots):
        get_w(jnp.int32(n)).start()

    barrier = pltpu.get_barrier_semaphore()

    def greet(k, _):
        pl.semaphore_signal(
            barrier, inc=1, device_id={"blk": lax.rem(me + k, nb), "group": g}, device_id_type=MESH
        )
        return 0

    lax.fori_loop(1, nb, greet, 0)
    for d in range(1, ng):
        pl.semaphore_signal(
            barrier, inc=1, device_id={"blk": me, "group": lax.rem(g + d, ng)}, device_id_type=MESH
        )

    for n in range(2):

        def fill(a, _):
            send_old[n, a] = caches[n][tab[a]]
            return 0

        lax.fori_loop(0, nb, fill, 0)
        recv_old[n][me] = send_old[n, me]
    pl.semaphore_wait(barrier, nb - 1 + ng - 1)

    def old_copy(n, k):
        a = lax.rem(me + k, nb)
        return remote(
            send_old.at[n, a], recv_old[n].at[me], s_old.at[n, a], r_old.at[n, me], a, g
        )

    def old_landed(n, k):
        a = lax.rem(me + nb - k, nb)
        return remote(send_old.at[n, a], recv_old[n].at[a], s_old.at[n, a], r_old.at[n, a], a, g)

    for n in range(2):

        def start_old(k, _):
            old_copy(n, k).start()
            return 0

        lax.fori_loop(1, nb, start_old, 0)

    def fresh_at(src, dst):
        return pl.ds(old_pages + mine * (src - dst), mine)

    def fresh_near(n):
        return remote(
            fresh[n], windows[n].at[fresh_at(g, partner)], s_fr.at[n, 0], r_fr.at[n, g], me, partner
        )

    def fresh_far(n):
        return remote(
            fresh[n], windows[n].at[fresh_at(g, across)], s_fr.at[n, 1], r_fr.at[n, g], me, across
        )

    def fresh_pass(n):
        return remote(
            windows[n].at[fresh_at(across, g)],
            windows[n].at[fresh_at(across, partner)],
            s_fr.at[n, 2],
            r_fr.at[n, across],
            me,
            partner,
        )

    def fresh_from(n, src):
        return remote(
            fresh[n], windows[n].at[fresh_at(src, g)], s_fr.at[n, 0], r_fr.at[n, src], me, partner
        )

    def quarter_to(n, dst):
        return remote(
            fresh[n].at[:, dst],
            qbuf.at[n, pl.ds(mine * g, mine)],
            s_q.at[n, dst],
            r_q.at[n, g],
            me,
            dst,
        )

    def quarter_from(n, src):
        return remote(
            fresh[n].at[:, g],
            qbuf.at[n, pl.ds(mine * src, mine)],
            s_q.at[n, g],
            r_q.at[n, src],
            me,
            partner,
        )

    def send_fresh(n):
        @pl.when(hi == 0)
        def _():
            fresh_far(n).start()

        @pl.when(core == 0)
        def _():
            fresh_near(n).start()

        for d in range(ng - 1):

            @pl.when(g > d)
            def _():
                quarter_to(n, d).start()

        windows[n][pl.ds(old_pages, mine)] = fresh[n][...]
        qbuf[n, pl.ds(mine * g, mine)] = fresh[n][:, g]

    send_fresh(1)

    tok = q_ref.shape[0]
    tiles = tok // tile
    first_pos = lengths[me] + g * tok
    positions = first_pos + lax.broadcasted_iota(jnp.int32, (tok, half), 0)
    angles = positions.astype(jnp.float32) * freq[...]
    lane = lax.broadcasted_iota(jnp.int32, (tok, half), 1)
    cos_ref[...] = jnp.cos(angles)
    sin_all = jnp.sin(angles)
    sin_ref[...] = jnp.where(lane < quarter, -sin_all, sin_all)

    def turn(lead, trows):
        lead = lead.astype(jnp.float32)
        turned = pltpu.roll(lead, quarter, axis=1)
        return (lead * cos_ref[trows, :] + turned * sin_ref[trows, :]).astype(jnp.bfloat16)

    for t in range(tiles):
        trows = pl.ds(t * tile, tile)
        lead = new_k[t, :, :, :half].reshape(tile, half)
        fresh_k[t, :, :, :half] = turn(lead, trows).reshape(ng, rows, half)
        fresh_k[t, :, :, half:] = new_k[t, :, :, half:]
    get_q.wait()
    for t in range(tiles):
        trows = pl.ds(t * tile, tile)
        for h in range(heads):
            roped = turn(q_ref[trows, h * hd : h * hd + half], trows)
            qs[t, h * tile : (h + 1) * tile, :half] = roped * scale
            qs[t, h * tile : (h + 1) * tile, half:] = (
                q_ref[trows, h * hd + half : (h + 1) * hd] * scale
            )
    send_fresh(0)
    att = q_ref

    def block(q, dst):
        return pl.ds(mine * (q - dst), mine)

    def ag_near(n, q):
        return remote(
            comp.at[n, pl.ds(mine * q, mine)],
            windows[n].at[block(q, partner), g],
            s_ag.at[n, q, 0],
            r_ag.at[n, q, g],
            me,
            partner,
        )

    def ag_far(n, q, dst):
        return remote(
            comp.at[n, pl.ds(mine * q, mine)],
            windows[n].at[block(q, dst), g],
            s_ag.at[n, q, 1],
            r_ag.at[n, q, g],
            me,
            dst,
        )

    def ag_pass(n, q):
        return remote(
            windows[n].at[block(q, g), across],
            windows[n].at[block(q, partner), across],
            s_ag.at[n, q, 2],
            r_ag.at[n, q, across],
            me,
            partner,
        )

    def ag_from(n, q, src):
        return remote(
            comp.at[n, pl.ds(mine * q, mine)],
            windows[n].at[block(q, g), src],
            s_ag.at[n, q, 0],
            r_ag.at[n, q, src],
            me,
            partner,
        )

    def far_do(n, q, act):
        @pl.when(other + 1 <= q)
        def _():
            act(ag_far(n, q, across))

        @pl.when(other == q)
        def _():
            act(ag_far(n, q, other))

    def start(c):
        c.start()

    def sent(c):
        c.wait_send()

    for n in range(2):

        def wait_old(k, _):
            old_landed(n, k).wait_recv()
            return 0

        lax.fori_loop(1, nb, wait_old, 0)

        def pack(j, _):
            comp[n, j] = recv_old[n][table[me, j] // pages_here]
            return 0

        lax.fori_loop(0, old_pages, pack, 0)
        for q in range(ng):
            far_do(n, q, start)

            @pl.when(partner <= q)
            def _():
                ag_near(n, q).start()

            @pl.when(g <= q)
            def _():
                windows[n][block(q, g), g] = comp[n, pl.ds(mine * q, mine)]

        if n == 0:

            @pl.when(hi == 1)
            def _():
                for m in range(2):
                    fresh_from(m, across).wait_recv()
                    fresh_pass(m).start()

    @pl.when(core == 1)
    def _():
        for n in range(2):
            fresh_from(n, partner).wait_recv()

    @pl.when(hi == 1)
    def _():
        for n in range(2):
            fresh_from(n, 1 - core).wait_recv()

    for src in range(ng):

        @pl.when(src < g)
        def _():
            for n in range(2):
                qbuf[n, pl.ds(mine * src, mine)] = windows[n][fresh_at(src, g), g]

        @pl.when(src > g)
        def _():
            for n in range(2):
                quarter_from(n, src).wait_recv()

    def fill_new(a, _):
        i = tab[nb + a]
        send_new[a, 0] = qbuf[0, i]
        send_new[a, 1] = qbuf[1, i]
        return 0

    lax.fori_loop(0, nb, fill_new, 0)

    def new_copy(k):
        a = lax.rem(me + k, nb)
        return remote(send_new.at[a], newrecv.at[me], s_new.at[a], r_new.at[me], a, g)

    def new_landed(k):
        a = lax.rem(me + nb - k, nb)
        return remote(send_new.at[a], newrecv.at[a], s_new.at[a], r_new.at[a], a, g)

    def start_new(k, _):
        new_copy(k).start()
        return 0

    newrecv[me] = send_new[me]

    for n in range(2):
        for q in range(ng):

            @pl.when(2 * hi + 1 <= q)
            def _():
                ag_from(n, q, across).wait_recv()
                ag_pass(n, q).start()

    for n in range(2):
        for q in range(ng):

            @pl.when(g <= q)
            def _():
                ag_from(n, q, partner).wait_recv()
                ag_from(n, q, other + 1 - core).wait_recv()

            @pl.when(2 * hi == q)
            def _():
                @pl.when(core == 0)
                def _():
                    ag_from(n, q, across).wait_recv()

    lax.fori_loop(1, nb, start_new, 0)

    parts = 5
    stack = heads // parts
    high = stack * tile
    span = old_pages + 1
    keys = span * tile
    empty = lengths[me] <= 0
    blank = [jnp.logical_and(empty, k + g < ng) for k in range(ng)]
    score = (score0, score1)
    prob = (prob0, prob1)
    sums = (sums0, sums1)
    r = lax.broadcasted_iota(jnp.int32, (tile, tile), 0)
    c = lax.broadcasted_iota(jnp.int32, (tile, tile), 1)
    after, upto = c > r, c <= r

    def scores(t, part, slot):
        score[slot][...] = lax.dot_general(
            qs[t, part * high : (part + 1) * high, :],
            kbuf[t : t + span].reshape(keys, hd),
            (((1,), (1,)), ((), ())),
            preferred_element_type=jnp.float32,
        )

    def softmax(t, part, slot):
        for h in range(stack):
            hrows = slice(h * tile, (h + 1) * tile)
            runs = []
            for k in range(ng + 1):
                begin, end = max(mine * k, t) - t, min(mine * (k + 1) - t, span)
                runs.append(
                    [score[slot][hrows, p * tile : (p + 1) * tile] for p in range(begin, end)]
                )
            runs[0][0] = jnp.where(after, runs[0][0], NEG)
            runs[-1][-1] = jnp.where(upto, runs[-1][-1], NEG)
            tops = [functools.reduce(jnp.maximum, run) for run in runs]
            for k in range(ng):
                tops[k] = jnp.where(blank[k], NEG, tops[k])
            m = jnp.max(functools.reduce(jnp.maximum, tops), axis=1, keepdims=True)
            p = total = 0
            for k, run in enumerate(runs):
                mk = jnp.where(blank[k], -NEG, m) if k < ng else m
                for x in run:
                    e = jnp.exp(x - mk)
                    total = total + e
                    prob[slot][hrows, p * tile : (p + 1) * tile] = e.astype(jnp.bfloat16)
                    p += 1
            sums[slot][hrows, :] = jnp.broadcast_to(
                jnp.sum(total, axis=1, keepdims=True), (tile, tile)
            )
        o = jnp.dot(
            prob[slot][...],
            vbuf[t : t + span].reshape(keys, hd),
            preferred_element_type=jnp.float32,
        )
        o = (o / sums[slot][:, :1]).astype(jnp.bfloat16)
        for h in range(stack):
            col = (part * stack + h) * hd
            att[t * tile : (t + 1) * tile, col : col + hd] = o[h * tile : (h + 1) * tile]

    steps = [(t, part) for t in range(tiles) for part in range(parts)]
    scores(*steps[0], 0)
    for i, at in enumerate(steps):
        if i + 1 < len(steps):
            scores(*steps[i + 1], (i + 1) % 2)
        softmax(*at, i % 2)

    def put(n):
        cols = pl.ds(pl.multiple_of(n * wide, wide), wide)
        return pltpu.make_async_copy(hid.at[lax.rem(n, 2)], hidden.at[:, cols], out_sem.at[n])

    def project(n, _):
        get_w(n).wait()

        @pl.when(n >= 2)
        def _():
            put(n - 2).wait()

        hid[lax.rem(n, 2)] = jnp.dot(
            att[...], wbuf[lax.rem(n, slots)], preferred_element_type=jnp.float32
        ).astype(jnp.bfloat16)
        put(n).start()

        @pl.when(n + slots < chunks)
        def _():
            get_w(n + slots).start()

        return 0

    lax.fori_loop(0, chunks - 1, project, 0)

    def wait_new(k, _):
        new_landed(k).wait_recv()
        return 0

    lax.fori_loop(1, nb, wait_new, 0)

    def update(p, _):
        b = tab[2 * nb + p] - 1
        for n in range(2):
            arrived = newrecv[jnp.maximum(b, 0), n]
            pages[n, p] = jnp.where(b >= 0, arrived, caches[n][p])
        return 0

    lax.fori_loop(0, pages_here, update, 0)
    outs = [
        pltpu.make_async_copy(pages.at[n], dst, loc.at[2 + n])
        for n, dst in enumerate((key_out, value_out))
    ]
    for x in outs:
        x.start()
    project(jnp.int32(chunks - 1), 0)

    def wait_rest(k, _):
        old_copy(0, k).wait_send()
        old_copy(1, k).wait_send()
        new_copy(k).wait_send()
        return 0

    lax.fori_loop(1, nb, wait_rest, 0)

    @pl.when(hi == 0)
    def _():
        for n in range(2):
            fresh_far(n).wait_send()

    @pl.when(core == 0)
    def _():
        for n in range(2):
            fresh_near(n).wait_send()

    @pl.when(hi == 1)
    def _():
        for n in range(2):
            fresh_pass(n).wait_send()

    for n in range(2):
        for d in range(ng - 1):

            @pl.when(g > d)
            def _():
                quarter_to(n, d).wait_send()

        for q in range(ng):
            far_do(n, q, sent)

            @pl.when(partner <= q)
            def _():
                ag_near(n, q).wait_send()

            @pl.when(2 * hi + 1 <= q)
            def _():
                ag_pass(n, q).wait_send()

    for n in range(chunks - 2, chunks):
        put(n).wait()
    for x in outs:
        x.wait()


def body(queries, new_keys, new_values, key_cache, value_cache, out_weight, lengths, page_table):
    nb = lax.axis_size("blk")
    ng = lax.axis_size("group")
    me = lax.axis_index("blk")
    tok = queries.shape[1]
    hd = new_keys.shape[2]
    heads = queries.shape[2] // hd
    pages_here, rows = key_cache.shape[:2]
    slots = page_table.shape[1]
    fresh = tok // rows
    old = slots - fresh
    mine = fresh // ng
    bf16 = jnp.bfloat16

    quarter = hd // 4
    freq = 10000.0 ** (-jnp.arange(quarter, dtype=jnp.float32) / quarter)
    freq = jnp.concatenate([freq, freq])[None]

    i32 = jnp.int32
    at = jnp.arange(2 * nb + pages_here, dtype=i32)[:, None, None]
    b = jnp.arange(nb, dtype=i32)[None, :, None]
    j = jnp.arange(slots, dtype=i32)[None, None, :]
    own, local = (page_table // pages_here)[None], (page_table % pages_here)[None]
    wants = (at == b) & (j < old) & (own == me)
    gives = (at >= nb) & (at < 2 * nb) & (b == me) & (j >= old) & (own == at - nb)
    takes = (j >= old) & (own == me) & (local == at - 2 * nb)
    tab = jnp.sum(
        jnp.where(wants, local, jnp.where(gives, j - old, jnp.where(takes, b + 1, 0))), axis=(1, 2)
    )

    shape4 = (mine, ng, rows, hd)
    tile = rows * ng
    keys = (old + 1) * tile
    width = heads * hd
    dma = pltpu.SemaphoreType.DMA
    vmem = pltpu.VMEM
    hidden, key_out, value_out = pl.pallas_call(
        functools.partial(layer_kernel, (nb, ng, old, mine, heads, hd, hd**-0.5)),
        out_shape=(
            jax.ShapeDtypeStruct((tok, out_weight.shape[1]), bf16),
            jax.ShapeDtypeStruct(key_cache.shape, bf16),
            jax.ShapeDtypeStruct(value_cache.shape, bf16),
        ),
        in_specs=[SM, SM, SM, VM, VM, VM, VM, VM, ANY, ANY],
        out_specs=(ANY, ANY, ANY),
        scratch_shapes=[
            vmem(shape4, bf16),
            vmem((tok, hd // 2), jnp.float32),
            vmem((tok, hd // 2), jnp.float32),
            vmem((tok, width), bf16),
            vmem((3, width, out_weight.shape[1] // 5), bf16),
            vmem((tok // tile, heads * tile, hd), bf16),
            vmem((2, tok, out_weight.shape[1] // 5), bf16),
            vmem((2, *key_cache.shape), bf16),
            vmem((nb, 2, rows, hd), bf16),
            vmem((old + mine, ng, rows, hd), bf16),
            vmem((old + mine, ng, rows, hd), bf16),
            vmem((2, nb, rows, hd), bf16),
            vmem((nb, rows, hd), bf16),
            vmem((nb, rows, hd), bf16),
            vmem((2, old, rows, hd), bf16),
            vmem((2, fresh, rows, hd), bf16),
            vmem((nb, 2, rows, hd), bf16),
            vmem((heads // 5 * tile, keys), jnp.float32),
            vmem((heads // 5 * tile, keys), jnp.float32),
            vmem((heads // 5 * tile, keys), bf16),
            vmem((heads // 5 * tile, keys), bf16),
            vmem((heads // 5 * tile, tile), jnp.float32),
            vmem((heads // 5 * tile, tile), jnp.float32),
            dma((2, nb)),
            dma((2, nb)),
            dma((2, 3)),
            dma((2, ng)),
            dma((2, ng)),
            dma((2, ng)),
            dma((2, ng, 3)),
            dma((2, ng, ng)),
            dma((nb,)),
            dma((nb,)),
            dma((4,)),
            dma((5,)),
            dma((3,)),
        ],
        compiler_params=pltpu.CompilerParams(
            collective_id=0, has_side_effects=True, vmem_limit_bytes=67_043_328
        ),
        name="layer",
    )(
        tab,
        page_table,
        lengths,
        freq,
        new_keys[0].reshape(shape4),
        new_values[0].reshape(shape4),
        key_cache,
        value_cache,
        queries[0],
        out_weight,
    )
    return (hidden[None], key_out, value_out)


def solution(mesh):
    split = P("blk", "group", None)
    return jax.shard_map(
        body,
        mesh=mesh,
        in_specs=(split, split, split, split, split, P(), P(), P()),
        out_specs=(split, split, split),
        check_vma=False,
    )
```

time: 109 us -> 85.7 us (0.79)
  the two profiles are of different devices: /device:TPU:75 before, /device:TPU:1 now
where the time goes in v3:
time: 85.7 us; the launch traced here: 85.4 us
  Pallas kernels  76.2 us (89%)
  local copies, waits for them, and re-layouts  5.18 us (6%)
  other arithmetic  3.36 us (4%)
    pallas_call x1, Pallas kernels, body(): pl.pallas_call(functools.partial(layer_kernel, (nb, ng, old, mine, heads,...  76.2 us
    unnamed x7, local copies, waits for them, and re-layouts  5.18 us

profile of v3, /device:TPU:1, one launch (start us, length us, event | category | flops | bytes accessed | tf_op | source)
XLA Modules:
  0.0 85.4 jit_solution(13588390777818840860)
XLA Ops:
  0.7 0.6 maximum_bitcast_fusion.freq
  1.3 0.1 iota_compare_fusion
  1.4 0.7 add_select_fusion
  2.1 0.7 broadcast_and_fusion
  2.8 1.2 %select_reduce_fusion.tab = s32[104]{0:T(128)} fusion(s32[32]{0:T(128)S(1)} %get-tuple-element.14, s32[104]{0:T(128)S(1)} %get-tuple-element.16, s32[32]{0:T(128)S(1)} %get-tuple-element.15, s32[104]{0:T(128)S(1)} %get-tuple-element.17, s32[32,32]{1,0:T(8,128)S(1)} %get-tuple-element.11, s32[32,32]{1,0:T(8,128)S(1)} %add_select_fusion, ...), kind=kLoop, calls=%fused_computation | loop fusion | flops 1171352 | bytes 18464 | tf_op jit(solution)/shard_map/reduce_sum | solution.py:596
  4.0 76.2 %layer.1 = (bf16[512,2560]{1,0:T(8,128)(2,1)}, bf16[40,32,256]{2,1,0:T(8,128)(2,1)}, bf16[40,32,256]{2,1,0:T(8,128)(2,1)}) custom-call(s32[104]{0:T(128)} %select_reduce_fusion.tab, s32[32,32]{1,0:T(8,128)} %table.1, s32[32]{0:T(128)} %lengths.1, f32[1,128]{1,0:T(1,128)} %maximum_bitcast_fusion.freq, bf16[4,4,32,256]{3,2,1,0:T(8,128)(2,1)} %bitcast.8, ...), custom_call_target="tpu_custom_call" | custom-call | tf_op jit(solution)/shard_map/layer/pallas_call | solution.py:606
  80.2 0.0 copy-start.1
  80.2 0.0 copy-start
  80.2 3.5 %copy.14 = bf16[1,512,2560]{2,1,0:T(8,128)(2,1)} copy(bf16[1,512,2560]{2,1,0:T(8,128)(2,1)} %bitcast.7) | data formatting | bytes 5242880
  83.7 0.0 copy-done.1
  83.7 0.8 copy.15
  84.6 0.0 copy-done
  84.6 0.8 copy.16
  (6 shorter events, 0.0 us)
Async XLA Ops:
  80.2 3.5 %copy-start.1 = (bf16[40,32,256]{2,1,0:T(8,128)(2,1)S(1)}, bf16[40,32,256]{2,1,0:T(8,128)(2,1)}, u32[]{:S(2)}) copy-start(bf16[40,32,256]{2,1,0:T(8,128)(2,1)} %get-tuple-element.24) | copy-start | bytes 1966084
  80.2 4.4 %copy-start = (bf16[40,32,256]{2,1,0:T(8,128)(2,1)S(1)}, bf16[40,32,256]{2,1,0:T(8,128)(2,1)}, u32[]{:S(2)}) copy-start(bf16[40,32,256]{2,1,0:T(8,128)(2,1)} %get-tuple-element.25) | copy-start | bytes 1966084

commit v4 on v3

--- a/solution.py
+++ b/solution.py
@@ -217,8 +217,6 @@
         windows[n][pl.ds(old_pages, mine)] = fresh[n][...]
         qbuf[n, pl.ds(mine * g, mine)] = fresh[n][:, g]
 
-    send_fresh(1)
-
     tok = q_ref.shape[0]
     tiles = tok // tile
     first_pos = lengths[me] + g * tok
@@ -248,7 +246,6 @@
             qs[t, h * tile : (h + 1) * tile, half:] = (
                 q_ref[trows, h * hd + half : (h + 1) * hd] * scale
             )
-    send_fresh(0)
     att = q_ref
 
     def block(q, dst):
@@ -334,12 +331,14 @@
                 windows[n][block(q, g), g] = comp[n, pl.ds(mine * q, mine)]
 
         if n == 0:
-
-            @pl.when(hi == 1)
-            def _():
-                for m in range(2):
-                    fresh_from(m, across).wait_recv()
-                    fresh_pass(m).start()
+            send_fresh(0)
+            send_fresh(1)
+
+    @pl.when(hi == 1)
+    def _():
+        for m in range(2):
+            fresh_from(m, across).wait_recv()
+            fresh_pass(m).start()
 
     @pl.when(core == 1)
     def _():
@@ -565,6 +564,31 @@
         put(n).wait()
     for x in outs:
         x.wait()
+
+
+def settle_kernel(parts, *refs):
+    n = len(refs) // 3
+    given, wanted, held = refs[:n], refs[n : 2 * n], refs[2 * n : 3 * n]
+    sem = refs[-1]
+    moves = []
+    for src, dst, buf, cuts in zip(given, wanted, held, parts):
+        size = src.shape[0] // cuts
+        for i in range(cuts):
+            at = pl.ds(i * size, size)
+            k = len(moves)
+            moves.append(
+                (
+                    pltpu.make_async_copy(src.at[at], buf.at[at], sem.at[0, k]),
+                    pltpu.make_async_copy(buf.at[at], dst.at[at], sem.at[1, k]),
+                )
+            )
+    for take, _ in moves:
+        take.start()
+    for take, give in moves:
+        take.wait()
+        give.start()
+    for _, give in moves:
+        give.wait()
 
 
 def body(queries, new_keys, new_values, key_cache, value_cache, out_weight, lengths, page_table):
@@ -666,6 +690,16 @@
         queries[0],
         out_weight,
     )
+    results = (hidden, key_out, value_out)
+    parts = (8, 2, 2)
+    hidden, key_out, value_out = pl.pallas_call(
+        functools.partial(settle_kernel, parts),
+        out_shape=tuple(jax.ShapeDtypeStruct(x.shape, x.dtype) for x in results),
+        in_specs=[ANY] * 3,
+        out_specs=(ANY,) * 3,
+        scratch_shapes=[*(vmem(x.shape, x.dtype) for x in results), dma((2, sum(parts)))],
+        name="settle",
+    )(*results)
     return (hidden[None], key_out, value_out)
 
 

time: 85.7 us -> 82.8 us (0.966)
  local copies, waits for them, and re-layouts: 5.18 us -> 0 us
  Pallas kernels: 76.2 us -> 78.4 us
    unnamed x7 -> x0, local copies, waits for them, and re-layouts: 5.18 us -> none
    pallas_call x0 -> x1, Pallas kernels: none -> 3.47 us  [body(): pl.pallas_call(functools.partial(settle_kernel, parts), out_shape=tuple((...]
    pallas_call x1, Pallas kernels: 76.2 us -> 74.9 us  [body(): pl.pallas_call(functools.partial(layer_kernel, (nb, ng, old, mine, heads,...]
where the time goes in v4:
time: 82.8 us; the launch traced here: 82.6 us
  Pallas kernels  78.4 us (95%)
  other arithmetic  3.36 us (4%)
  between operations  0.85 us (1%)
    pallas_call x1, Pallas kernels, body(): pl.pallas_call(functools.partial(layer_kernel, (nb, ng, old, mine, heads,...  74.9 us
    pallas_call x1, Pallas kernels, body(): pl.pallas_call(functools.partial(settle_kernel, parts), out_shape=tuple((...  3.47 us

profile of v4, /device:TPU:1, one launch (start us, length us, event | category | flops | bytes accessed | tf_op | source)
XLA Modules:
  0.0 82.6 jit_solution(1129249904760165064)
XLA Ops:
  0.7 0.6 maximum_bitcast_fusion.freq
  1.3 0.1 iota_compare_fusion
  1.4 0.7 add_select_fusion
  2.1 0.7 broadcast_and_fusion
  2.8 1.2 %select_reduce_fusion.tab = s32[104]{0:T(128)} fusion(s32[32]{0:T(128)S(1)} %get-tuple-element.20, s32[104]{0:T(128)S(1)} %get-tuple-element.22, s32[32]{0:T(128)S(1)} %get-tuple-element.21, s32[104]{0:T(128)S(1)} %get-tuple-element.23, s32[32,32]{1,0:T(8,128)S(1)} %get-tuple-element.17, s32[32,32]{1,0:T(8,128)S(1)} %add_select_fusion, ...), kind=kLoop, calls=%fused_computation | loop fusion | flops 1171352 | bytes 18464 | tf_op jit(solution)/shard_map/reduce_sum | solution.py:620
  4.0 74.9 %layer.1 = (bf16[512,2560]{1,0:T(8,128)(2,1)}, bf16[40,32,256]{2,1,0:T(8,128)(2,1)}, bf16[40,32,256]{2,1,0:T(8,128)(2,1)}) custom-call(s32[104]{0:T(128)} %select_reduce_fusion.tab, s32[32,32]{1,0:T(8,128)} %table.1, s32[32]{0:T(128)} %lengths.1, f32[1,128]{1,0:T(1,128)} %maximum_bitcast_fusion.freq, bf16[4,4,32,256]{3,2,1,0:T(8,128)(2,1)} %bitcast.7, ...), custom_call_target="tpu_custom_call" | custom-call | tf_op jit(solution)/shard_map/layer/pallas_call | solution.py:630
  78.9 3.5 %settle.1 = (bf16[512,2560]{1,0:T(8,128)(2,1)}, bf16[40,32,256]{2,1,0:T(8,128)(2,1)}, bf16[40,32,256]{2,1,0:T(8,128)(2,1)}) custom-call(bf16[512,2560]{1,0:T(8,128)(2,1)} %get-tuple-element.9.refs_0_, bf16[40,32,256]{2,1,0:T(8,128)(2,1)} %get-tuple-element.10.refs_1_, bf16[40,32,256]{2,1,0:T(8,128)(2,1)} %get-tuple-element.11.refs_2_), custom_call_target="tpu_custom_call" | custom-call | tf_op jit(solution)/shard_map/settle/pallas_call | solution.py:695
  (6 shorter events, 0.0 us)
